TPU v7x, 512 devices: a whole 4x4x16 slice. The times are simulated.
512 devices in a mesh: leaf: 16 (over z), col: 32 (over y, x, core).
Axes of the slice: x: 4, y: 4, z: 16, core: 2. Of those that a mesh axis runs over, the one named last changes fastest.
Arguments:
- leaf_solution: float32 [16, 16384, 256], P('leaf', 'col'), may hold values from -6 to 6
- coupling: float32 [16, 768, 128, 128], P('leaf', 'col'), may hold values from -0.01953125 to 0.01953125
- tile_slot: int32 [16, 768], P('leaf', 'col'), may hold values from 0 to 63, as said below
- sep_rhs: float32 [2048, 256], P('col'), may hold values from -6 to 6
- pivot_inverse: float32 [16, 128, 128], P('leaf'), as said below
Outputs:
- sep_solution: float32 [2048, 256], P('col')
- leaf_update: float32 [16, 16384, 256], P('leaf', 'col')
Inputs may be any that keep to these rules, and one draw needn't show every extreme that they name: `tile_slot`: within each aligned block of 24 entries along dimension 1 the values are distinct. `pivot_inverse`: each block is symmetric.
All inputs are finite; a program needn't handle non-finite values.
Results may differ from a plain program's by a relative error of at most 0.0003.
Values sent between devices are 32-bit elements; how exact they have to be, the bound alone decides.
No kernel may reach another device: no remote copies, remote signals or barrier semaphores. Data moves between devices by JAX's collectives and lax.ppermute only.
A program may use at most 64 MiB of HBM per device.

v0:
```python
import jax
import jax.numpy as jnp
from jax import lax
from jax.sharding import PartitionSpec as P


def on_device(leaf_solution, coupling, tile_slot, sep_rhs, pivot_inverse):
    precise = lax.Precision.HIGHEST
    tile_size = coupling.shape[-1]
    rhs_count = leaf_solution.shape[-1]
    leaf_rows = leaf_solution.shape[1]
    col_blocks = leaf_rows // tile_size
    own_rows = sep_rhs.shape[0]
    sep_rows = own_rows * lax.axis_size("col")
    row_blocks = sep_rows // tile_size
    tile_data = coupling[0]
    slot_ids = tile_slot[0]
    tile_row = slot_ids // col_blocks
    tile_col = slot_ids % col_blocks
    leaf_blocks = leaf_solution[0].reshape(col_blocks, tile_size, rhs_count)
    picked = leaf_blocks[tile_col]
    products = jnp.einsum("tij,tjk->tik", tile_data, picked, precision=precise)
    row_hot = (tile_row[None, :] == jnp.arange(row_blocks, dtype=jnp.int32)[:, None]).astype(
        jnp.float32
    )
    partial_value = -jnp.einsum("nt,tik->nik", row_hot, products, precision=precise).reshape(
        sep_rows, rhs_count
    )
    rhs_term = jnp.where(lax.axis_index("leaf") == 0, sep_rhs, jnp.zeros_like(sep_rhs))
    placed = lax.dynamic_update_slice_in_dim(
        jnp.zeros_like(partial_value), rhs_term, lax.axis_index("col") * own_rows, 0
    )
    partial_value = partial_value + placed
    summed = lax.psum(partial_value, ("leaf", "col"))
    pivots = lax.all_gather(pivot_inverse, "leaf", axis=0, tiled=True)
    solved = jnp.einsum(
        "bij,bjk->bik", pivots, summed.reshape(row_blocks, tile_size, rhs_count), precision=precise
    )
    solution = solved.reshape(sep_rows, rhs_count)
    sep_blocks = solution.reshape(row_blocks, tile_size, rhs_count)
    chosen = sep_blocks[tile_row]
    transposed = jnp.einsum("tij,tik->tjk", tile_data, chosen, precision=precise)
    col_hot = (tile_col[None, :] == jnp.arange(col_blocks, dtype=jnp.int32)[:, None]).astype(
        jnp.float32
    )
    update = jnp.einsum("ct,tjk->cjk", col_hot, transposed, precision=precise)
    leaf_update = (leaf_blocks - update).reshape(1, leaf_rows, rhs_count)
    sep_solution = lax.dynamic_slice_in_dim(solution, lax.axis_index("col") * own_rows, own_rows, 0)
    return (sep_solution, leaf_update)


def solution(mesh):
    return jax.shard_map(
        on_device,
        mesh=mesh,
        in_specs=(
            P("leaf", "col", None),
            P("leaf", "col", None, None),
            P("leaf", "col"),
            P("col", None),
            P("leaf", None, None),
        ),
        out_specs=(P("col", None), P("leaf", "col", None)),
        check_vma=False,
    )
```

profile of v0, /device:TPU:1, one launch (start us, length us, event | category | flops | bytes accessed | tf_op | source)
XLA Modules:
  0.0 554.2 jit_solution(7920181868726836255)
XLA Ops:
  8.0 0.0 copy-start
  8.0 0.0 all-reduce.2.cloned.1.call-start
  8.1 0.8 fusion.11
  8.8 0.7 fusion.9
  9.5 3.5 gather_fusion
  13.0 8.3 %convolution_bitcast_fusion.1 = f32[24,128,256]{1,2,0:T(8,128)} fusion(f32[24,128,256]{2,1,0:T(8,128)} %gather_fusion, f32[1,24,128,128]{3,2,1,0:T(8,128)S(1)} %copy-done), kind=kOutput, calls=%fused_computation.3 | convolution fusion | flops 1207959552 | bytes 7864320 | tf_op jit(solution)/shard_map/tij,tjk->tik/dot_general | solution.py:22
  21.3 3.6 copy.18
  24.8 3.3 convolution_negate_fusion
  28.1 0.0 copy-start.3
  28.1 2.5 copy.19
  30.6 0.0 copy-done.3
  30.6 1.5 add_dynamic-update-slice_fusion
  32.1 0.0 all-reduce.2.cloned.1.call-update
  32.1 0.2 all-gather.2.cloned.1.call-start
  32.4 0.3 all-gather.2.cloned.1.call-update
  32.7 488.4 %all-reduce.2.cloned.1.call-done = f32[16,128,256]{2,1,0:T(8,128)} async-done(((f32[16,128,256]{2,1,0:T(8,128)}), f32[16,128,256]{2,1,0:T(8,128)}) %all-reduce.2.cloned.1.call-update) | async-done | bytes 2097168 | tf_op jit(solution)/shard_map/psum | solution.py:34
  521.1 3.8 fusion.13
  525.0 1.3 copy-done.2
  526.3 0.6 constant_dynamic-slice_fusion
  526.9 4.0 gather_fusion.1
  530.9 8.3 %convolution_bitcast_fusion = f32[24,128,256]{1,2,0:T(8,128)} fusion(f32[24,128,256]{2,1,0:T(8,128)} %gather_fusion.1, f32[1,24,128,128]{3,2,1,0:T(8,128)S(1)} %copy-done), kind=kOutput, calls=%fused_computation.2 | convolution fusion | flops 1207959552 | bytes 7864320 | tf_op jit(solution)/shard_map/tij,tik->tjk/dot_general | solution.py:42
  539.2 3.6 copy.21
  542.7 3.2 fusion.6
  545.9 0.9 copy_subtract_fusion
  (7 shorter events, 0.0 us)
Async XLA Ops:
  8.0 5.0 copy-start
  8.0 513.1 %all-reduce.2.cloned.1.call-start = ((), (), s32[]{:S(2)}) async-start(), calls=%async_computation | async-start | bytes 4194304 | tf_op jit(solution)/shard_map/psum | solution.py:34
  28.1 2.5 copy-start.3
  32.1 489.0 %all-gather.2.cloned.1.call-start = ((), (), s32[]{:S(2)}) async-start(), calls=%async_computation.1 | async-start | bytes 1114112 | tf_op jit(solution)/shard_map/all_gather | solution.py:35
  525.0 1.3 copy-start.2
  542.7 3.2 copy-start.1
Sparse Core Ops, SparseCore 0:
  32.3 488.7 all-reduce.1
Sparse Core Ops, SparseCore 1:
  34.7 66.8 all-gather.1
where the time goes:
time: 555 us; the launch traced here: 554 us
  waiting for transfers between devices  489 us (88%)
  matrix products  26.8 us (5%)
  local copies, waits for them, and re-layouts  19.1 us (3%)
  between operations  15.5 us (3%)
    psum x1, waiting for transfers between devices, on_device(): summed = lax.psum(partial_value, ('leaf', 'col'))  488 us
  transfers between devices with their start and end apart: 2, of which 1 were waited for; matrix products, arithmetic and copies ran while one was open for 0% of the time, Pallas kernels for 0%

commit v1 on v0

v1 whole, which is shorter than its diff:
```python
import jax
import jax.numpy as jnp
from jax import lax
from jax.experimental import pallas as pl
from jax.experimental.pallas import tpu as pltpu
from jax.sharding import Mesh, PartitionSpec as P

F32 = jnp.float32
BF16 = jnp.bfloat16


def split(value):
    high = value.astype(BF16)
    low = (value - high.astype(F32)).astype(BF16)
    return high, low


def forward_kernel(info, slots, leaf, tiles, rhs, own, send, lhs):
    z, chip, core = info[0], info[1], info[2]
    count, size = tiles.shape[0], tiles.shape[1]
    col_blocks = leaf.shape[0] // size
    slabs = own.shape[0]
    halves = ((own, pl.multiple_of(core * size, size)), (send, pl.multiple_of((1 - core) * size, size)))
    lane = lax.broadcasted_iota(jnp.int32, (size, size), 1)
    keep = (lane // (size // 2) == core) & (z == 0)
    for part, (out, start) in enumerate(halves):
        out[...] = jnp.zeros_like(out)
        piece = rhs[:, pl.ds(start, size)]
        placed = jnp.where(keep, jnp.concatenate([piece, piece], 0).T, 0.0)
        out[:, chip] = placed.reshape(slabs, 8, size)
        for b in range(col_blocks):
            high, low = split(leaf[b * size : (b + 1) * size, pl.ds(start, size)].T)
            lhs[b, part * size : (part + 1) * size] = jnp.concatenate([high, high, low], 1)

    def product(t):
        high, low = split(tiles[t])
        weights = jnp.concatenate([high, low, high], 1)
        return lax.dot_general(
            lhs[slots[t] % col_blocks], weights, (((1,), (1,)), ((), ())), preferred_element_type=F32
        )

    def add(t, value):
        row = slots[t] // col_blocks
        own[:, row] -= value[:size].reshape(slabs, 8, size)
        send[:, row] -= value[size:].reshape(slabs, 8, size)

    ahead = product(0)
    for t in range(count):
        value = ahead
        if t + 1 < count:
            ahead = product(t + 1)
        add(t, value)


def solve_kernel(parts, pivot, out):
    total = jnp.sum(parts[...], 0)
    solved = jnp.dot(total, pivot[0], preferred_element_type=F32, precision=lax.Precision.HIGHEST)
    out[...] = jnp.broadcast_to(solved[None], out.shape)


def backward_kernel(info, slots, leaf, tiles, own, other, sep_out, leaf_out, lhs, update, turned):
    chip, core = info[1], info[2]
    count, size = tiles.shape[0], tiles.shape[1]
    col_blocks = leaf.shape[0] // size
    row_blocks = own.shape[1]
    halves = ((own, pl.multiple_of(core * size, size)), (other, pl.multiple_of((1 - core) * size, size)))
    update[...] = jnp.zeros_like(update)
    for part, (ref, start) in enumerate(halves):
        turned[:, pl.ds(start, size)] = ref[:, chip].reshape(size, size).T
        for k in range(row_blocks):
            high, low = split(ref[:, k].reshape(size, size))
            lhs[k, part * size : (part + 1) * size] = jnp.concatenate([high, high, low], 1)
    rows = sep_out.shape[0]
    sep_out[...] = turned[pl.ds(pl.multiple_of(core * rows, rows), rows), :]

    def product(t):
        high, low = split(tiles[t])
        weights = jnp.concatenate([high, low, high], 0)
        return jnp.dot(lhs[slots[t] // col_blocks], weights, preferred_element_type=F32)

    ahead = product(0)
    for t in range(count):
        value = ahead
        if t + 1 < count:
            ahead = product(t + 1)
        update[slots[t] % col_blocks] += value
    for b in range(col_blocks):
        rows_b = slice(b * size, (b + 1) * size)
        for part, (_, start) in enumerate(halves):
            change = update[b, part * size : (part + 1) * size].T
            leaf_out[rows_b, pl.ds(start, size)] = leaf[rows_b, pl.ds(start, size)] - change


def on_device(leaf_solution, coupling, tile_slot, sep_rhs, pivot_inverse):
    n_z, n_x = lax.axis_size("z"), lax.axis_size("x")
    n_chip = lax.axis_size("y") * n_x
    leaf, tiles, slots = leaf_solution[0], coupling[0], tile_slot[0]
    size = tiles.shape[-1]
    count = tiles.shape[0]
    row_blocks = n_z
    col_blocks = leaf.shape[0] // size
    rhs_count = leaf.shape[1]
    core = lax.axis_index("c")
    info = jnp.stack([lax.axis_index("z"), lax.axis_index("y") * n_x + lax.axis_index("x"), core]).astype(jnp.int32)
    smem = pl.BlockSpec(memory_space=pltpu.SMEM)
    vmem = pl.BlockSpec(memory_space=pltpu.VMEM)
    part = jax.ShapeDtypeStruct((n_chip, row_blocks, 8, size), F32)
    own, send = pl.pallas_call(
        forward_kernel,
        out_shape=(part, part),
        in_specs=[smem, smem, vmem, vmem, vmem],
        out_specs=(vmem, vmem),
        scratch_shapes=[pltpu.VMEM((col_blocks, rhs_count, 3 * size), BF16)],
        name="forward",
    )(info, slots, leaf, tiles, sep_rhs)
    swap = [(0, 1), (1, 0)]
    half = own + lax.ppermute(send, "c", swap)
    shared = lax.all_to_all(half, ("y", "x"), 0, 0, tiled=True)
    slab = jnp.sum(shared, 0)
    parts = lax.all_to_all(slab, "z", 0, 0, tiled=True)
    copies = pl.pallas_call(
        solve_kernel,
        out_shape=jax.ShapeDtypeStruct(parts.shape, F32),
        in_specs=[vmem, vmem],
        out_specs=vmem,
        name="solve",
    )(parts, pivot_inverse)
    blocks = lax.all_to_all(copies, "z", 0, 0, tiled=True)
    wide = jnp.broadcast_to(blocks[None], (n_chip,) + blocks.shape)
    mine = lax.all_to_all(wide, ("y", "x"), 0, 0, tiled=True)
    other = lax.ppermute(mine, "c", swap)
    sep_solution, leaf_update = pl.pallas_call(
        backward_kernel,
        out_shape=(jax.ShapeDtypeStruct(sep_rhs.shape, F32), jax.ShapeDtypeStruct(leaf.shape, F32)),
        in_specs=[smem, smem, vmem, vmem, vmem, vmem],
        out_specs=(vmem, vmem),
        scratch_shapes=[
            pltpu.VMEM((row_blocks, rhs_count, 3 * size), BF16),
            pltpu.VMEM((col_blocks, rhs_count, size), F32),
            pltpu.VMEM((size, rhs_count), F32),
        ],
        name="backward",
    )(info, slots, leaf, tiles, mine, other)
    return sep_solution, leaf_update[None]


def solution(mesh):
    chips = mesh.devices.reshape(mesh.shape["leaf"], 4, mesh.shape["col"] // 8, 2)
    fine = Mesh(chips, ("z", "y", "x", "c"))
    col = ("y", "x", "c")
    return jax.shard_map(
        on_device,
        mesh=fine,
        in_specs=(P("z", col, None), P("z", col, None, None), P("z", col), P(col, None), P("z", None, None)),
        out_specs=(P(col, None), P("z", col, None)),
        check_vma=False,
    )
```

time: 555 us -> 111 us (0.20)
  waiting for transfers between devices: 489 us -> 4.74 us
  blocking collectives: 0 us -> 75.6 us
  matrix products: 26.8 us -> 0 us
  local copies, waits for them, and re-layouts: 19.1 us -> 1.11 us
  starting transfers between devices: 0.26 us -> 15.6 us
  between operations: 15.5 us -> 0.67 us
  Pallas kernels: 0 us -> 11.2 us
    psum x1 -> x0, waiting for transfers between devices: 488 us -> none  [on_device(): summed = lax.psum(partial_value, ('leaf', 'col'))]
    all_to_all x0 -> x4, blocking collectives: none -> 75.6 us  [the longest x1 24.7 us: on_device(): parts = lax.all_to_all(slab, 'z', 0, 0, tiled=True)]
    dot_general x5 -> x0, matrix products: 26.8 us -> none  [the longest x1 8.28 us: on_device(): products = jnp.einsum('tij,tjk->tik', tile_data, picked, precision=precise)]
    ppermute x0 -> x2, starting transfers between devices: none -> 15.6 us  [the longest x1 8.73 us: on_device(): half = own + lax.ppermute(send, 'c', swap)]
    pallas_call x0 -> x3, Pallas kernels: none -> 11.2 us  [the longest x1 4.92 us: on_device(): pl.pallas_call(backward_kernel, out_shape=(jax.ShapeDtypeStruct(sep_rhs.s...]
    gather x2 -> x0, local copies, waits for them, and re-layouts: 7.45 us -> none  [the longest x1 3.97 us: on_device(): chosen = sep_blocks[tile_row]]
    dot_general x2 -> x0, local copies, waits for them, and re-layouts: 7.12 us -> none  [the longest x1 3.56 us: on_device(): products = jnp.einsum('tij,tjk->tik', tile_data, picked, precision=precise)]
  transfers between devices with their start and end apart: 2 -> 2, of which waited for: 1 -> 2; matrix products, arithmetic and copies ran while one was open for 0% -> 0% of each run, Pallas kernels for 0% -> 0%
where the time goes in v1:
time: 111 us
  blocking collectives  75.6 us (68%)
  starting transfers between devices  15.6 us (14%)
  Pallas kernels  11.2 us (10%)
  waiting for transfers between devices  4.74 us (4%)
  other arithmetic  2.04 us (2%)
  local copies, waits for them, and re-layouts  1.11 us (1%)
    all_to_all x1, blocking collectives, on_device(): parts = lax.all_to_all(slab, 'z', 0, 0, tiled=True)  24.7 us
    all_to_all x1, blocking collectives, on_device(): shared = lax.all_to_all(half, ('y', 'x'), 0, 0, tiled=True)  19.3 us
    all_to_all x1, blocking collectives, on_device(): mine = lax.all_to_all(wide, ('y', 'x'), 0, 0, tiled=True)  16.5 us
    all_to_all x1, blocking collectives, on_device(): blocks = lax.all_to_all(copies, 'z', 0, 0, tiled=True)  15.1 us
    ppermute x1, starting transfers between devices, on_device(): half = own + lax.ppermute(send, 'c', swap)  8.73 us
    ppermute x1, starting transfers between devices, on_device(): other = lax.ppermute(mine, 'c', swap)  6.87 us
    pallas_call x1, Pallas kernels, on_device(): pl.pallas_call(backward_kernel, out_shape=(jax.ShapeDtypeStruct(sep_rhs.s...  4.92 us
    pallas_call x1, Pallas kernels, on_device(): pl.pallas_call(forward_kernel, out_shape=(part, part), in_specs=[smem, sm...  4.58 us
  transfers between devices with their start and end apart: 2, of which 2 were waited for; matrix products, arithmetic and copies ran while one was open for 0% of the time, Pallas kernels for 0%

profile of v1, /device:TPU:1, one launch (start us, length us, event | category | flops | bytes accessed | tf_op | source)
XLA Modules:
  0.0 110.9 jit_solution(506802831012779480)
XLA Ops:
  0.6 0.6 pad_add_fusion.info
  1.3 4.6 %forward.1 = (f32[16,16,8,128]{3,2,1,0:T(8,128)}, f32[16,16,8,128]{3,2,1,0:T(8,128)}) custom-call(s32[3]{0:T(128)} %pad_add_fusion.info, s32[24]{0:T(128)} %bitcast.11, f32[512,256]{1,0:T(8,128)} %bitcast.9, f32[24,128,128]{2,1,0:T(8,128)} %bitcast.7, f32[64,256]{1,0:T(8,128)} %rhs.1), custom_call_target="tpu_custom_call" | custom-call | tf_op jit(solution)/shard_map/forward/pallas_call | solution.py:108
  5.9 8.7 %collective-permute-start = (f32[16,16,8,128]{3,2,1,0:T(8,128)}, f32[16,16,8,128]{3,2,1,0:T(8,128)S(1)}, u32[]{:S(2)}, u32[]{:S(2)}) collective-permute-start(f32[16,16,8,128]{3,2,1,0:T(8,128)} %get-tuple-element.7), channel_id=1, source_target_pairs={{0,1},{1,0},{2,3},{3,2},{4,5},{5,4},{6,7},{7,6},{8,9},{9,8},{10,11... | collective-permute-start | bytes 3145736 | tf_op jit(solution)/shard_map/ppermute | solution.py:117
  14.6 2.5 %collective-permute-done = f32[16,16,8,128]{3,2,1,0:T(8,128)S(1)} collective-permute-done((f32[16,16,8,128]{3,2,1,0:T(8,128)}, f32[16,16,8,128]{3,2,1,0:T(8,128)S(1)}, u32[]{:S(2)}, u32[]{:S(2)}) %collective-permute-start) | collective-permute-done | bytes 1048608 | tf_op jit(solution)/shard_map/ppermute | solution.py:117
  17.1 1.3 %add.7 = f32[16,16,8,128]{3,2,1,0:T(8,128)S(1)} add(f32[16,16,8,128]{3,2,1,0:T(8,128)} %get-tuple-element.6, f32[16,16,8,128]{3,2,1,0:T(8,128)S(1)} %collective-permute-done) | non-fusion elementwise | flops 262144 | bytes 3145728 | tf_op jit(solution)/shard_map/add | solution.py:117
  18.4 19.3 %all_to_all.20 = f32[16,16,8,128]{3,2,1,0:T(8,128)S(1)} all-to-all(f32[16,16,8,128]{3,2,1,0:T(8,128)S(1)} %add.7), channel_id=1, replica_groups=mesh['z'=16,'y'=4,'x'=4,'c'=2] {'y','x'}, dimensions={0} | all-to-all | bytes 2097152 | tf_op jit(solution)/shard_map/all_to_all | solution.py:118
  37.7 0.1 reduce_sum.9
  37.7 24.7 %all_to_all.21.parts = f32[16,8,128]{2,1,0:T(8,128)} all-to-all(f32[16,8,128]{2,1,0:T(8,128)S(1)} %reduce_sum.9), channel_id=1, replica_groups=mesh['z'=16,'y'=4,'x'=4,'c'=2] {'z'}, dimensions={0} | all-to-all | bytes 131072 | tf_op jit(solution)/shard_map/all_to_all | solution.py:120
  62.4 1.7 %solve.1 = f32[16,8,128]{2,1,0:T(8,128)} custom-call(f32[16,8,128]{2,1,0:T(8,128)} %all_to_all.21.parts, f32[1,128,128]{2,1,0:T(8,128)} %pivot.1), custom_call_target="tpu_custom_call" | custom-call | tf_op jit(solution)/shard_map/solve/pallas_call | solution.py:121
  64.1 15.1 %all_to_all.22 = f32[16,8,128]{2,1,0:T(8,128)S(1)} all-to-all(f32[16,8,128]{2,1,0:T(8,128)} %solve.1), channel_id=1, replica_groups=mesh['z'=16,'y'=4,'x'=4,'c'=2] {'z'}, dimensions={0} | all-to-all | bytes 131072 | tf_op jit(solution)/shard_map/all_to_all | solution.py:128
  79.2 0.1 broadcast_in_dim.4
  79.3 16.5 %all_to_all.23.own = f32[16,16,8,128]{3,2,1,0:T(8,128)S(1)} all-to-all(f32[16,16,8,128]{3,2,1,0:T(8,128)S(1)} %broadcast_in_dim.4), channel_id=1, replica_groups=mesh['z'=16,'y'=4,'x'=4,'c'=2] {'y','x'}, dimensions={0} | all-to-all | bytes 2097152 | tf_op jit(solution)/shard_map/all_to_all | solution.py:130
  95.8 0.0 copy-start
  95.8 6.9 %collective-permute-start.1 = (f32[16,16,8,128]{3,2,1,0:T(8,128)S(1)}, f32[16,16,8,128]{3,2,1,0:T(8,128)S(1)}, u32[]{:S(2)}, u32[]{:S(2)}) collective-permute-start(f32[16,16,8,128]{3,2,1,0:T(8,128)S(1)} %all_to_all.23.own), channel_id=1, source_target_pairs={{0,1},{1,0},{2,3},{3,2},{4,5},{5,4},{6,7},{7,6},{8,9},{9,8},{10,11... | collective-permute-start | bytes 3145736 | tf_op jit(solution)/shard_map/ppermute | solution.py:131
  102.7 2.3 %collective-permute-done.1.other = f32[16,16,8,128]{3,2,1,0:T(8,128)S(1)} collective-permute-done((f32[16,16,8,128]{3,2,1,0:T(8,128)S(1)}, f32[16,16,8,128]{3,2,1,0:T(8,128)S(1)}, u32[]{:S(2)}, u32[]{:S(2)}) %collective-permute-start.1) | collective-permute-done | bytes 1048608 | tf_op jit(solution)/shard_map/ppermute | solution.py:131
  105.0 0.0 copy-done
  105.0 0.0 copy-start.1
  105.0 1.0 copy-done.1
  106.0 4.9 %backward.1 = (f32[64,256]{1,0:T(8,128)}, f32[512,256]{1,0:T(8,128)}) custom-call(s32[3]{0:T(128)} %pad_add_fusion.info, s32[24]{0:T(128)} %bitcast.12, f32[512,256]{1,0:T(8,128)} %bitcast.10, f32[24,128,128]{2,1,0:T(8,128)} %bitcast.8, f32[16,16,8,128]{3,2,1,0:T(8,128)} %copy-done, f32[16,16,8,128]{3,2,1,0:T(8,128)} %copy-done.1), custom_call_target="tpu_custom_call" | custom-call | tf_op jit(solution)/shard_map/backward/pallas_call | solution.py:132
Async XLA Ops:
  5.9 11.2 %collective-permute-start = (f32[16,16,8,128]{3,2,1,0:T(8,128)}, f32[16,16,8,128]{3,2,1,0:T(8,128)S(1)}, u32[]{:S(2)}, u32[]{:S(2)}) collective-permute-start(f32[16,16,8,128]{3,2,1,0:T(8,128)} %get-tuple-element.7), channel_id=1, source_target_pairs={{0,1},{1,0},{2,3},{3,2},{4,5},{5,4},{6,7},{7,6},{8,9},{9,8},{10,11... | collective-permute-start | bytes 3145736 | tf_op jit(solution)/shard_map/ppermute | solution.py:117
  95.8 9.1 %copy-start = (f32[16,16,8,128]{3,2,1,0:T(8,128)}, f32[16,16,8,128]{3,2,1,0:T(8,128)S(1)}, u32[]{:S(2)}) copy-start(f32[16,16,8,128]{3,2,1,0:T(8,128)S(1)} %all_to_all.23.own) | copy-start | bytes 3145732
  95.8 9.1 %collective-permute-start.1 = (f32[16,16,8,128]{3,2,1,0:T(8,128)S(1)}, f32[16,16,8,128]{3,2,1,0:T(8,128)S(1)}, u32[]{:S(2)}, u32[]{:S(2)}) collective-permute-start(f32[16,16,8,128]{3,2,1,0:T(8,128)S(1)} %all_to_all.23.own), channel_id=1, source_target_pairs={{0,1},{1,0},{2,3},{3,2},{4,5},{5,4},{6,7},{7,6},{8,9},{9,8},{10,11... | collective-permute-start | bytes 3145736 | tf_op jit(solution)/shard_map/ppermute | solution.py:131
  105.0 1.0 copy-start.1

commit v2 on v1

v2 whole, which is shorter than its diff:
```python
from functools import partial

import jax
import jax.numpy as jnp
from jax import lax
from jax.experimental import pallas as pl
from jax.experimental.pallas import tpu as pltpu
from jax.sharding import Mesh, PartitionSpec as P

F32 = jnp.float32
BF16 = jnp.bfloat16


def split(value):
    high = value.astype(BF16)
    low = (value - high.astype(F32)).astype(BF16)
    return high, low


def place():
    return lax.axis_index("z"), lax.axis_index("y") * lax.axis_size("x") + lax.axis_index("x"), lax.axis_index("c")


def half_start(core, size):
    return pl.multiple_of(core * size, size)


def chunk_copies(source, target, sems):
    step = source.shape[0] // sems.shape[0]
    chunks = [pl.ds(i * step, step) for i in range(sems.shape[0])]
    copies = [pltpu.make_async_copy(source.at[c], target.at[c], sems.at[i]) for i, c in enumerate(chunks)]
    for copy in copies:
        copy.start()
    return copies


def pipelined(copies, count, product, use):
    step = count // len(copies)
    ahead = None
    for t in range(count + 1):
        value = ahead
        if t < count:
            if t % step == 0:
                copies[t // step].wait()
            ahead = product(t)
        if t > 0:
            use(t - 1, value)


def forward_kernel(swapped, slots, leaf, tiles_hbm, rhs, out, lhs, tiles, sems):
    copies = chunk_copies(tiles_hbm, tiles, sems)
    z, chip, core = place()
    count, size = tiles.shape[0], tiles.shape[1]
    col_blocks = leaf.shape[0] // size
    slabs = out.shape[0]
    start = half_start(1 - core if swapped else core, size)
    lane = lax.broadcasted_iota(jnp.int32, (size, size), 1)
    keep = (lane // (size // 2) == core) & (z == 0)
    out[...] = jnp.zeros_like(out)
    piece = rhs[:, pl.ds(start, size)]
    placed = jnp.where(keep, jnp.concatenate([piece, piece], 0).T, 0.0)
    out[:, chip] = placed.reshape(slabs, 8, size)
    for b in range(col_blocks):
        high, low = split(leaf[b * size : (b + 1) * size, pl.ds(start, size)].T)
        lhs[b] = jnp.concatenate([high, high, low], 1)

    def product(t):
        high, low = split(tiles[t])
        weights = jnp.concatenate([high, low, high], 1)
        return lax.dot_general(
            lhs[slots[t] % col_blocks], weights, (((1,), (1,)), ((), ())), preferred_element_type=F32
        )

    def use(t, value):
        out[:, slots[t] // col_blocks] -= value.reshape(slabs, 8, size)

    pipelined(copies, count, product, use)


def solve_kernel(parts, pivot, out):
    total = jnp.sum(parts[...], 0)
    solved = jnp.dot(total, pivot[0], preferred_element_type=F32, precision=lax.Precision.HIGHEST)
    out[...] = jnp.broadcast_to(solved[None], out.shape)


def backward_half(swapped, slots, leaf_hbm, tiles_hbm, sol, to, sep_out, leaf_out, lhs, update, tiles, sems, leaf, leaf_sem):
    copies = chunk_copies(tiles_hbm, tiles, sems)
    leaf_copy = pltpu.make_async_copy(leaf_hbm, leaf, leaf_sem)
    leaf_copy.start()
    _, chip, core = place()
    count, size = tiles.shape[0], tiles.shape[1]
    col_blocks = leaf.shape[0] // size
    row_blocks = sol.shape[1]
    cols = pl.ds(half_start(1 - core if swapped else core, size), size)
    update[...] = jnp.zeros_like(update)
    for k in range(row_blocks):
        high, low = split(sol[:, k].reshape(size, size))
        lhs[k] = jnp.concatenate([high, high, low], 1)
    rows = sep_out.shape[0]
    turned = sol[:, chip].reshape(size, size).T
    to = cols if to is None else to
    sep_out[:, to] = jnp.where(core == 0, turned[:rows], turned[rows:])

    def product(t):
        high, low = split(tiles[t])
        weights = jnp.concatenate([high, low, high], 0)
        return jnp.dot(lhs[slots[t] // col_blocks], weights, preferred_element_type=F32)

    def use(t, value):
        update[slots[t] % col_blocks] += value

    pipelined(copies, count, product, use)
    leaf_copy.wait()
    for b in range(col_blocks):
        rows_b = slice(b * size, (b + 1) * size)
        leaf_out[rows_b, to] = leaf[rows_b, cols] - update[b].T


def backward_own(slots, leaf, tiles, sol, *rest):
    backward_half(False, slots, leaf, tiles, sol, slice(None), *rest)


def backward_other(slots, leaf, tiles, sol, sep_part, leaf_part, sep_out, leaf_out, *rest):
    size = tiles.shape[1]
    cols = pl.ds(half_start(place()[2], size), size)
    sep_out[:, cols] = sep_part[...]
    leaf_out[:, cols] = leaf_part[...]
    backward_half(True, slots, leaf, tiles, sol, None, sep_out, leaf_out, *rest)


def in_vmem(array):
    return pltpu.with_memory_space_constraint(array, pltpu.VMEM)


def on_device(leaf_solution, coupling, tile_slot, sep_rhs, pivot_inverse):
    n_z = lax.axis_size("z")
    n_chip = lax.axis_size("y") * lax.axis_size("x")
    slots = tile_slot[0]
    leaf, tiles, rhs, pivot = leaf_solution[0], coupling[0], sep_rhs, in_vmem(pivot_inverse)
    size = tiles.shape[-1]
    col_blocks = leaf.shape[0] // size
    smem = pl.BlockSpec(memory_space=pltpu.SMEM)
    vmem = pl.BlockSpec(memory_space=pltpu.VMEM)
    hbm = pl.BlockSpec(memory_space=pl.ANY)
    staging = [pltpu.VMEM(tiles.shape, F32), pltpu.SemaphoreType.DMA((4,))]

    def forward(swapped):
        return pl.pallas_call(
            partial(forward_kernel, swapped),
            out_shape=pltpu.VMEM((n_chip, n_z, 8, size), F32),
            in_specs=[smem, vmem, hbm, vmem],
            out_specs=vmem,
            scratch_shapes=[pltpu.VMEM((col_blocks, size, 3 * size), BF16)] + staging,
            name="forward_send" if swapped else "forward_own",
        )(slots, leaf, tiles, rhs)

    swap = [(0, 1), (1, 0)]
    arrived = lax.ppermute(forward(True), "c", swap)
    half = forward(False) + arrived
    shared = lax.all_to_all(half, ("y", "x"), 0, 0, tiled=True)
    slab = jnp.sum(shared, 0)
    parts = lax.all_to_all(slab, "z", 0, 0, tiled=True)
    copies = pl.pallas_call(
        solve_kernel,
        out_shape=pltpu.VMEM(parts.shape, F32),
        in_specs=[vmem, vmem],
        out_specs=vmem,
        name="solve",
    )(in_vmem(parts), pivot)
    blocks = lax.all_to_all(copies, "z", 0, 0, tiled=True)
    wide = jnp.broadcast_to(blocks[None], (n_chip,) + blocks.shape)
    mine = lax.all_to_all(wide, ("y", "x"), 0, 0, tiled=True)
    other = lax.ppermute(mine, "c", swap)
    scratch = [pltpu.VMEM((n_z, size, 3 * size), BF16), pltpu.VMEM((col_blocks, size, size), F32)]
    scratch += staging + [pltpu.VMEM(leaf.shape, F32), pltpu.SemaphoreType.DMA]
    parts_own = pl.pallas_call(
        backward_own,
        out_shape=(pltpu.VMEM((rhs.shape[0], size), F32), pltpu.VMEM((leaf.shape[0], size), F32)),
        in_specs=[smem, hbm, hbm, vmem],
        out_specs=(vmem, vmem),
        scratch_shapes=scratch,
        name="backward_own",
    )(slots, leaf, tiles, in_vmem(mine))
    sep_solution, leaf_update = pl.pallas_call(
        backward_other,
        out_shape=(jax.ShapeDtypeStruct(rhs.shape, F32), jax.ShapeDtypeStruct(leaf.shape, F32)),
        in_specs=[smem, hbm, hbm, vmem, vmem, vmem],
        out_specs=(vmem, vmem),
        scratch_shapes=scratch,
        name="backward_other",
    )(slots, leaf, tiles, in_vmem(other), *map(in_vmem, parts_own))
    return sep_solution, leaf_update[None]


def solution(mesh):
    chips = mesh.devices.reshape(mesh.shape["leaf"], 4, mesh.shape["col"] // 8, 2)
    fine = Mesh(chips, ("z", "y", "x", "c"))
    col = ("y", "x", "c")
    return jax.shard_map(
        on_device,
        mesh=fine,
        in_specs=(P("z", col, None), P("z", col, None, None), P("z", col), P(col, None), P("z", None, None)),
        out_specs=(P(col, None), P("z", col, None)),
        check_vma=False,
    )
```

time: 111 us -> 107 us (0.964)
  waiting for transfers between devices: 4.74 us -> 0.01 us
  Pallas kernels: 11.2 us -> 14.8 us
  other arithmetic: 2.04 us -> 0.19 us
    pallas_call x3 -> x5, Pallas kernels: 11.2 us -> 14.8 us  [the longest x2 7.52 us: forward(): pl.pallas_call(partial(forward_kernel, swapped), out_shape=pltpu.VMEM((n_...]
    ppermute x1, waiting for transfers between devices: 2.48 us -> 0.01 us  [on_device(): arrived = lax.ppermute(forward(True), 'c', swap)]
    ppermute x1, waiting for transfers between devices: 2.26 us -> 0.01 us  [on_device(): other = lax.ppermute(mine, 'c', swap)]
    add x1, other arithmetic: 1.34 us -> 0.13 us  [on_device(): half = forward(False) + arrived]
  transfers between devices with their start and end apart: 2 -> 2, of which waited for: 2 -> 0; matrix products, arithmetic and copies ran while one was open for 0% -> 0% of each run, Pallas kernels for 0% -> 7%
where the time goes in v2:
time: 107 us
  blocking collectives  76.1 us (71%)
  starting transfers between devices  15 us (14%)
  Pallas kernels  14.8 us (14%)
    all_to_all x1, blocking collectives, on_device(): parts = lax.all_to_all(slab, 'z', 0, 0, tiled=True)  24.6 us
    all_to_all x1, blocking collectives, on_device(): shared = lax.all_to_all(half, ('y', 'x'), 0, 0, tiled=True)  19.7 us
    all_to_all x1, blocking collectives, on_device(): mine = lax.all_to_all(wide, ('y', 'x'), 0, 0, tiled=True)  17.4 us
    all_to_all x1, blocking collectives, on_device(): blocks = lax.all_to_all(copies, 'z', 0, 0, tiled=True)  14.4 us
    ppermute x1, starting transfers between devices, on_device(): arrived = lax.ppermute(forward(True), 'c', swap)  8.75 us
    pallas_call x2, Pallas kernels, forward(): pl.pallas_call(partial(forward_kernel, swapped), out_shape=pltpu.VMEM((n_...  7.52 us
    ppermute x1, starting transfers between devices, on_device(): other = lax.ppermute(mine, 'c', swap)  6.29 us
    pallas_call x1, Pallas kernels, on_device(): pl.pallas_call(backward_other, out_shape=(jax.ShapeDtypeStruct(rhs.shape,...  3.87 us
  transfers between devices with their start and end apart: 2, of which 0 were waited for; matrix products, arithmetic and copies ran while one was open for 0% of the time, Pallas kernels for 7%

profile of v2, /device:TPU:1, one launch (start us, length us, event | category | flops | bytes accessed | tf_op | source)
XLA Modules:
  0.0 106.9 jit_solution(10801134148351960495)
XLA Ops:
  0.6 3.8 %forward_send.1 = f32[16,16,8,128]{3,2,1,0:T(8,128)S(1)} custom-call(s32[24]{0:T(128)} %bitcast.12, f32[512,256]{1,0:T(8,128)} %bitcast.8, f32[24,128,128]{2,1,0:T(8,128)} %bitcast.4, f32[64,256]{1,0:T(8,128)} %rhs.3), custom_call_target="tpu_custom_call" | custom-call | tf_op jit(solution)/shard_map/forward_send/pallas_call | solution.py:148
  4.4 8.7 %collective-permute-start = (f32[16,16,8,128]{3,2,1,0:T(8,128)S(1)}, f32[16,16,8,128]{3,2,1,0:T(8,128)S(1)}, u32[]{:S(2)}, u32[]{:S(2)}) collective-permute-start(f32[16,16,8,128]{3,2,1,0:T(8,128)S(1)} %forward_send.1), channel_id=1, source_target_pairs={{0,1},{1,0},{2,3},{3,2},{4,5},{5,4},{6,7},{7,6},{8,9},{9,8},{10,11... | collective-permute-start | bytes 3145736 | tf_op jit(solution)/shard_map/ppermute | solution.py:158
  13.1 3.8 %forward_own.1 = f32[16,16,8,128]{3,2,1,0:T(8,128)S(1)} custom-call(s32[24]{0:T(128)} %bitcast.13, f32[512,256]{1,0:T(8,128)} %bitcast.9, f32[24,128,128]{2,1,0:T(8,128)} %bitcast.5, f32[64,256]{1,0:T(8,128)} %rhs.3), custom_call_target="tpu_custom_call" | custom-call | tf_op jit(solution)/shard_map/forward_own/pallas_call | solution.py:148
  16.9 0.0 collective-permute-done
  16.9 0.1 add.3
  17.1 0.0 copy-start
  17.1 19.7 %all_to_all.20 = f32[16,16,8,128]{3,2,1,0:T(8,128)S(1)} all-to-all(f32[16,16,8,128]{3,2,1,0:T(8,128)S(1)} %add.3), channel_id=1, replica_groups=mesh['z'=16,'y'=4,'x'=4,'c'=2] {'y','x'}, dimensions={0} | all-to-all | bytes 2097152 | tf_op jit(solution)/shard_map/all_to_all | solution.py:160
  36.8 0.1 reduce_sum.9
  36.9 24.6 %all_to_all.21.parts = f32[16,8,128]{2,1,0:T(8,128)S(1)} all-to-all(f32[16,8,128]{2,1,0:T(8,128)S(1)} %reduce_sum.9), channel_id=1, replica_groups=mesh['z'=16,'y'=4,'x'=4,'c'=2] {'z'}, dimensions={0} | all-to-all | bytes 131072 | tf_op jit(solution)/shard_map/all_to_all | solution.py:162
  61.5 0.0 copy-done
  61.5 0.2 solve.1
  61.6 14.4 %all_to_all.22 = f32[16,8,128]{2,1,0:T(8,128)S(1)} all-to-all(f32[16,8,128]{2,1,0:T(8,128)S(1)} %solve.1), channel_id=1, replica_groups=mesh['z'=16,'y'=4,'x'=4,'c'=2] {'z'}, dimensions={0} | all-to-all | bytes 131072 | tf_op jit(solution)/shard_map/all_to_all | solution.py:170
  76.0 0.1 broadcast_in_dim.4
  76.1 17.4 %all_to_all.23.sol = f32[16,16,8,128]{3,2,1,0:T(8,128)S(1)} all-to-all(f32[16,16,8,128]{3,2,1,0:T(8,128)S(1)} %broadcast_in_dim.4), channel_id=1, replica_groups=mesh['z'=16,'y'=4,'x'=4,'c'=2] {'y','x'}, dimensions={0} | all-to-all | bytes 2097152 | tf_op jit(solution)/shard_map/all_to_all | solution.py:172
  93.5 6.3 %collective-permute-start.1 = (f32[16,16,8,128]{3,2,1,0:T(8,128)S(1)}, f32[16,16,8,128]{3,2,1,0:T(8,128)S(1)}, u32[]{:S(2)}, u32[]{:S(2)}) collective-permute-start(f32[16,16,8,128]{3,2,1,0:T(8,128)S(1)} %all_to_all.23.sol), channel_id=1, source_target_pairs={{0,1},{1,0},{2,3},{3,2},{4,5},{5,4},{6,7},{7,6},{8,9},{9,8},{10,11... | collective-permute-start | bytes 3145736 | tf_op jit(solution)/shard_map/ppermute | solution.py:173
  99.8 3.2 %backward_own.1 = (f32[64,128]{1,0:T(8,128)S(1)}, f32[512,128]{1,0:T(8,128)S(1)}) custom-call(s32[24]{0:T(128)} %bitcast.14, f32[512,256]{1,0:T(8,128)} %bitcast.10, f32[24,128,128]{2,1,0:T(8,128)} %bitcast.6, f32[16,16,8,128]{3,2,1,0:T(8,128)S(1)} %all_to_all.23.sol), custom_call_target="tpu_custom_call" | custom-call | tf_op jit(solution)/shard_map/backward_own/pallas_call | solution.py:176
  103.1 0.0 collective-permute-done.1.sol
  103.1 3.9 %backward_other.1 = (f32[64,256]{1,0:T(8,128)}, f32[512,256]{1,0:T(8,128)}) custom-call(s32[24]{0:T(128)} %bitcast.15, f32[512,256]{1,0:T(8,128)} %bitcast.11, f32[24,128,128]{2,1,0:T(8,128)} %bitcast.7, f32[16,16,8,128]{3,2,1,0:T(8,128)S(1)} %collective-permute-done.1.sol, f32[64,128]{1,0:T(8,128)S(1)} %get-tuple-element.6.sep_part, ...), custom_call_target="tpu_custom_call" | custom-call | tf_op jit(solution)/shard_map/backward_other/pallas_call | solution.py:184
Async XLA Ops:
  4.4 12.5 %collective-permute-start = (f32[16,16,8,128]{3,2,1,0:T(8,128)S(1)}, f32[16,16,8,128]{3,2,1,0:T(8,128)S(1)}, u32[]{:S(2)}, u32[]{:S(2)}) collective-permute-start(f32[16,16,8,128]{3,2,1,0:T(8,128)S(1)} %forward_send.1), channel_id=1, source_target_pairs={{0,1},{1,0},{2,3},{3,2},{4,5},{5,4},{6,7},{7,6},{8,9},{9,8},{10,11... | collective-permute-start | bytes 3145736 | tf_op jit(solution)/shard_map/ppermute | solution.py:158
  17.1 44.4 %copy-start = (f32[1,128,128]{2,1,0:T(8,128)S(1)}, f32[1,128,128]{2,1,0:T(8,128)}, u32[]{:S(2)}) copy-start(f32[1,128,128]{2,1,0:T(8,128)} %pivot.1) | copy-start | bytes 196612
  93.5 9.5 %collective-permute-start.1 = (f32[16,16,8,128]{3,2,1,0:T(8,128)S(1)}, f32[16,16,8,128]{3,2,1,0:T(8,128)S(1)}, u32[]{:S(2)}, u32[]{:S(2)}) collective-permute-start(f32[16,16,8,128]{3,2,1,0:T(8,128)S(1)} %all_to_all.23.sol), channel_id=1, source_target_pairs={{0,1},{1,0},{2,3},{3,2},{4,5},{5,4},{6,7},{7,6},{8,9},{9,8},{10,11... | collective-permute-start | bytes 3145736 | tf_op jit(solution)/shard_map/ppermute | solution.py:173

commit v3 on v2

v3 whole, which is shorter than its diff:
```python
from functools import partial

import jax
import jax.numpy as jnp
from jax import lax
from jax.experimental import pallas as pl
from jax.experimental.pallas import tpu as pltpu
from jax.sharding import Mesh, PartitionSpec as P

F32 = jnp.float32
BF16 = jnp.bfloat16
CHUNKS = (8, 16)


def split(value):
    high = value.astype(BF16)
    low = (value - high.astype(F32)).astype(BF16)
    return high, low


def place():
    return lax.axis_index("z"), lax.axis_index("y") * lax.axis_size("x") + lax.axis_index("x"), lax.axis_index("c")


def half_columns(core, size):
    return pl.ds(pl.multiple_of(core * size, size), size)


def start_copies(pairs, tiles_hbm, tiles, sems):
    parts = [pl.ds(sum(CHUNKS[:i]), step) for i, step in enumerate(CHUNKS)]
    pairs = pairs + [(tiles_hbm.at[part], tiles.at[part]) for part in parts]
    copies = [pltpu.make_async_copy(source, target, sems.at[i]) for i, (source, target) in enumerate(pairs)]
    for copy in copies:
        copy.start()
    return copies[: -len(CHUNKS)], copies[-len(CHUNKS) :]


def pipelined(copies, count, product, use):
    first = {sum(CHUNKS[:i]): copy for i, copy in enumerate(copies)}
    ahead = None
    for t in range(count + 1):
        value = ahead
        if t < count:
            if t in first:
                first[t].wait()
            ahead = product(t)
        if t > 0:
            use(t - 1, value)


def forward_kernel(swapped, slots_hbm, leaf_hbm, tiles_hbm, rhs_hbm, out, lhs, tiles, slots, leaf, rhs, sems):
    z, chip, core = place()
    count, size = tiles.shape[0], tiles.shape[1]
    col_blocks = leaf.shape[0] // size
    slabs = out.shape[0]
    cols = half_columns(1 - core if swapped else core, size)
    small, copies = start_copies(
        [(leaf_hbm.at[:, cols], leaf), (slots_hbm, slots), (rhs_hbm.at[:, cols], rhs)], tiles_hbm, tiles, sems
    )
    out[...] = jnp.zeros_like(out)
    small[0].wait()
    for b in range(col_blocks):
        high, low = split(leaf[b * size : (b + 1) * size].T)
        lhs[b] = jnp.concatenate([high, high, low], 1)
    small[1].wait()
    small[2].wait()
    lane = lax.broadcasted_iota(jnp.int32, (size, size), 1)
    keep = (lane // (size // 2) == core) & (z == 0)
    placed = jnp.where(keep, jnp.concatenate([rhs[...], rhs[...]], 0).T, 0.0)
    out[:, chip] = placed.reshape(slabs, 8, size)

    def product(t):
        high, low = split(tiles[t])
        weights = jnp.concatenate([high.T, low.T, high.T], 0)
        return jnp.dot(lhs[slots[t] % col_blocks], weights, preferred_element_type=F32)

    def use(t, value):
        out[:, slots[t] // col_blocks] -= value.reshape(slabs, 8, size)

    pipelined(copies, count, product, use)


def solve_kernel(parts, pivot, out):
    total = jnp.sum(parts[...], 0)
    solved = jnp.dot(total, pivot[0], preferred_element_type=F32, precision=lax.Precision.HIGHEST)
    out[...] = jnp.broadcast_to(solved[None], out.shape)


def backward_half(swapped, slots_hbm, leaf_hbm, weights, sol, sep_out, leaf_out, lhs, update, sep, leaf, slots, sems):
    _, chip, core = place()
    count, size = weights.shape[0], sol.shape[-1]
    col_blocks = leaf.shape[0] // size
    row_blocks = sol.shape[1]
    cols = half_columns(1 - core if swapped else core, size)
    slots_in = pltpu.make_async_copy(slots_hbm, slots, sems.at[0])
    leaf_in = pltpu.make_async_copy(leaf_hbm.at[:, cols], leaf, sems.at[1])
    sep_back = pltpu.make_async_copy(sep, sep_out.at[:, cols], sems.at[2])
    leaf_back = pltpu.make_async_copy(leaf, leaf_out.at[:, cols], sems.at[3])
    slots_in.start()
    leaf_in.start()
    update[...] = jnp.zeros_like(update)
    rows = sep.shape[0]
    turned = sol[:, chip].reshape(size, size).T
    sep[...] = jnp.where(core == 0, turned[:rows], turned[rows:])
    sep_back.start()
    for k in range(row_blocks):
        high, low = split(sol[:, k].reshape(size, size))
        lhs[k] = jnp.concatenate([high, high, low], 1)
    slots_in.wait()

    def product(t):
        return jnp.dot(lhs[slots[t] // col_blocks], weights[t], preferred_element_type=F32)

    ahead = product(0)
    for t in range(count):
        value = ahead
        if t + 1 < count:
            ahead = product(t + 1)
        update[slots[t] % col_blocks] += value
    leaf_in.wait()
    for b in range(col_blocks):
        rows_b = slice(b * size, (b + 1) * size)
        leaf[rows_b] -= update[b].T
    leaf_back.start()
    sep_back.wait()
    leaf_back.wait()


def backward_own(slots, leaf, tiles_hbm, sol, sep_out, leaf_out, weights, tiles, tiles_sem, *rest):
    copy = pltpu.make_async_copy(tiles_hbm, tiles, tiles_sem)
    copy.start()
    copy.wait()
    for t in range(tiles.shape[0]):
        high, low = split(tiles[t])
        weights[t] = jnp.concatenate([high, low, high], 0)
    backward_half(False, slots, leaf, weights, sol, sep_out, leaf_out, *rest)


def backward_other(slots, leaf, weights, sol, sep_part, leaf_part, sep_out, leaf_out, *rest):
    backward_half(True, slots, leaf, weights, sol, sep_out, leaf_out, *rest)


def in_vmem(array):
    return pltpu.with_memory_space_constraint(array, pltpu.VMEM)


def on_device(leaf_solution, coupling, tile_slot, sep_rhs, pivot_inverse):
    n_z = lax.axis_size("z")
    n_chip = lax.axis_size("y") * lax.axis_size("x")
    slots, leaf, tiles, rhs, pivot = tile_slot[0], leaf_solution[0], coupling[0], sep_rhs, in_vmem(pivot_inverse)
    size = tiles.shape[-1]
    leaf_rows, sep_rows = leaf.shape[0], rhs.shape[0]
    col_blocks = leaf_rows // size
    vmem = pl.BlockSpec(memory_space=pltpu.VMEM)
    hbm = pl.BlockSpec(memory_space=pl.ANY)
    staging = [pltpu.VMEM(tiles.shape, F32), pltpu.SMEM(slots.shape, jnp.int32), pltpu.VMEM((leaf_rows, size), F32)]

    def forward(swapped):
        return pl.pallas_call(
            partial(forward_kernel, swapped),
            out_shape=pltpu.VMEM((n_chip, n_z, 8, size), F32),
            in_specs=[hbm, hbm, hbm, hbm],
            out_specs=vmem,
            scratch_shapes=[pltpu.VMEM((col_blocks, size, 3 * size), BF16)]
            + staging
            + [pltpu.VMEM((sep_rows, size), F32), pltpu.SemaphoreType.DMA((3 + len(CHUNKS),))],
            name="forward_send" if swapped else "forward_own",
        )(slots, leaf, tiles, rhs)

    swap = [(0, 1), (1, 0)]
    arrived = lax.ppermute(forward(True), "c", swap)
    half = forward(False) + arrived
    shared = lax.all_to_all(half, ("y", "x"), 0, 0, tiled=True)
    slab = jnp.sum(shared, 0)
    parts = lax.all_to_all(slab, "z", 0, 0, tiled=True)
    copies = pl.pallas_call(
        solve_kernel,
        out_shape=pltpu.VMEM(parts.shape, F32),
        in_specs=[vmem, vmem],
        out_specs=vmem,
        name="solve",
    )(in_vmem(parts), pivot)
    blocks = lax.all_to_all(copies, "z", 0, 0, tiled=True)
    wide = jnp.broadcast_to(blocks[None], (n_chip,) + blocks.shape)
    mine = lax.all_to_all(wide, ("y", "x"), 0, 0, tiled=True)
    other = lax.ppermute(mine, "c", swap)
    scratch = [
        pltpu.VMEM((n_z, size, 3 * size), BF16),
        pltpu.VMEM((col_blocks, size, size), F32),
        pltpu.VMEM((sep_rows, size), F32),
        pltpu.VMEM((leaf_rows, size), F32),
        pltpu.SMEM(slots.shape, jnp.int32),
        pltpu.SemaphoreType.DMA((4,)),
    ]
    results = (jax.ShapeDtypeStruct(rhs.shape, F32), jax.ShapeDtypeStruct(leaf.shape, F32))
    sep_part, leaf_part, weights = pl.pallas_call(
        backward_own,
        out_shape=results + (pltpu.VMEM((tiles.shape[0], 3 * size, size), BF16),),
        in_specs=[hbm, hbm, hbm, vmem],
        out_specs=(hbm, hbm, vmem),
        scratch_shapes=[pltpu.VMEM(tiles.shape, F32), pltpu.SemaphoreType.DMA] + scratch,
        compiler_params=pltpu.CompilerParams(vmem_limit_bytes=12 << 20),
        name="backward_own",
    )(slots, leaf, tiles, in_vmem(mine))
    sep_solution, leaf_update = pl.pallas_call(
        backward_other,
        out_shape=results,
        in_specs=[hbm, hbm, vmem, vmem, hbm, hbm],
        out_specs=(hbm, hbm),
        scratch_shapes=scratch,
        input_output_aliases={4: 0, 5: 1},
        compiler_params=pltpu.CompilerParams(vmem_limit_bytes=12 << 20),
        name="backward_other",
    )(slots, leaf, in_vmem(weights), in_vmem(other), sep_part, leaf_part)
    return sep_solution, leaf_update[None]


def solution(mesh):
    chips = mesh.devices.reshape(mesh.shape["leaf"], 4, mesh.shape["col"] // 8, 2)
    fine = Mesh(chips, ("z", "y", "x", "c"))
    col = ("y", "x", "c")
    return jax.shard_map(
        on_device,
        mesh=fine,
        in_specs=(P("z", col, None), P("z", col, None, None), P("z", col), P(col, None), P("z", None, None)),
        out_specs=(P(col, None), P("z", col, None)),
        check_vma=False,
    )
```

time: 107 us -> 102 us (0.953)
  Pallas kernels: 14.8 us -> 9.52 us
  blocking collectives: 76.1 us -> 75 us
    pallas_call x2, Pallas kernels: 7.52 us -> 4.76 us  [forward(): pl.pallas_call(partial(forward_kernel, swapped), out_shape=pltpu.VMEM((n_...]
    pallas_call x2, Pallas kernels: 7.11 us -> 4.59 us  [the longest x1 2.36 us: on_device(): pl.pallas_call(backward_own, out_shape=results + (pltpu.VMEM((tiles.shape...]
  transfers between devices with their start and end apart: 2 -> 2, of which waited for: 0 -> 0; matrix products, arithmetic and copies ran while one was open for 0% -> 0% of each run, Pallas kernels for 7% -> 5%
where the time goes in v3:
time: 102 us; the launch traced here: 101 us
  blocking collectives  75 us (74%)
  starting transfers between devices  15.6 us (15%)
  Pallas kernels  9.52 us (9%)
    all_to_all x1, blocking collectives, on_device(): parts = lax.all_to_all(slab, 'z', 0, 0, tiled=True)  24.7 us
    all_to_all x1, blocking collectives, on_device(): shared = lax.all_to_all(half, ('y', 'x'), 0, 0, tiled=True)  19.5 us
    all_to_all x1, blocking collectives, on_device(): mine = lax.all_to_all(wide, ('y', 'x'), 0, 0, tiled=True)  16.4 us
    all_to_all x1, blocking collectives, on_device(): blocks = lax.all_to_all(copies, 'z', 0, 0, tiled=True)  14.4 us
    ppermute x1, starting transfers between devices, on_device(): arrived = lax.ppermute(forward(True), 'c', swap)  8.75 us
    ppermute x1, starting transfers between devices, on_device(): other = lax.ppermute(mine, 'c', swap)  6.8 us
    pallas_call x2, Pallas kernels, forward(): pl.pallas_call(partial(forward_kernel, swapped), out_shape=pltpu.VMEM((n_...  4.76 us
    pallas_call x1, Pallas kernels, on_device(): pl.pallas_call(backward_own, out_shape=results + (pltpu.VMEM((tiles.shape...  2.36 us
  transfers between devices with their start and end apart: 2, of which 0 were waited for; matrix products, arithmetic and copies ran while one was open for 0% of the time, Pallas kernels for 5%

profile of v3, /device:TPU:1, one launch (start us, length us, event | category | flops | bytes accessed | tf_op | source)
XLA Modules:
  0.0 101.2 jit_solution(13001264406375996784)
XLA Ops:
  0.6 2.4 %forward_send.1 = f32[16,16,8,128]{3,2,1,0:T(8,128)S(1)} custom-call(s32[24]{0:T(128)} %bitcast.11, f32[512,256]{1,0:T(8,128)} %bitcast.7, f32[24,128,128]{2,1,0:T(8,128)} %bitcast.4, f32[64,256]{1,0:T(8,128)} %rhs_hbm.3), custom_call_target="tpu_custom_call" | custom-call | tf_op jit(solution)/shard_map/forward_send/pallas_call | solution.py:159
  3.0 8.8 %collective-permute-start = (f32[16,16,8,128]{3,2,1,0:T(8,128)S(1)}, f32[16,16,8,128]{3,2,1,0:T(8,128)S(1)}, u32[]{:S(2)}, u32[]{:S(2)}) collective-permute-start(f32[16,16,8,128]{3,2,1,0:T(8,128)S(1)} %forward_send.1), channel_id=1, source_target_pairs={{0,1},{1,0},{2,3},{3,2},{4,5},{5,4},{6,7},{7,6},{8,9},{9,8},{10,11... | collective-permute-start | bytes 3145736 | tf_op jit(solution)/shard_map/ppermute | solution.py:171
  11.8 2.4 %forward_own.1 = f32[16,16,8,128]{3,2,1,0:T(8,128)S(1)} custom-call(s32[24]{0:T(128)} %bitcast.12, f32[512,256]{1,0:T(8,128)} %bitcast.8, f32[24,128,128]{2,1,0:T(8,128)} %bitcast.5, f32[64,256]{1,0:T(8,128)} %rhs_hbm.3), custom_call_target="tpu_custom_call" | custom-call | tf_op jit(solution)/shard_map/forward_own/pallas_call | solution.py:159
  14.2 0.0 collective-permute-done
  14.2 0.1 add.3
  14.3 0.0 copy-start.2
  14.3 19.5 %all_to_all.20 = f32[16,16,8,128]{3,2,1,0:T(8,128)S(1)} all-to-all(f32[16,16,8,128]{3,2,1,0:T(8,128)S(1)} %add.3), channel_id=1, replica_groups=mesh['z'=16,'y'=4,'x'=4,'c'=2] {'y','x'}, dimensions={0} | all-to-all | bytes 2097152 | tf_op jit(solution)/shard_map/all_to_all | solution.py:173
  33.8 0.0 copy-start
  33.8 0.0 copy-start.1
  33.8 0.0 copy-start.3
  33.8 0.1 reduce_sum.9
  33.9 24.7 %all_to_all.21.parts = f32[16,8,128]{2,1,0:T(8,128)S(1)} all-to-all(f32[16,8,128]{2,1,0:T(8,128)S(1)} %reduce_sum.9), channel_id=1, replica_groups=mesh['z'=16,'y'=4,'x'=4,'c'=2] {'z'}, dimensions={0} | all-to-all | bytes 131072 | tf_op jit(solution)/shard_map/all_to_all | solution.py:175
  58.6 0.0 copy-done.2
  58.6 0.2 solve.1
  58.8 14.4 %all_to_all.22 = f32[16,8,128]{2,1,0:T(8,128)S(1)} all-to-all(f32[16,8,128]{2,1,0:T(8,128)S(1)} %solve.1), channel_id=1, replica_groups=mesh['z'=16,'y'=4,'x'=4,'c'=2] {'z'}, dimensions={0} | all-to-all | bytes 131072 | tf_op jit(solution)/shard_map/all_to_all | solution.py:183
  73.2 0.1 broadcast_in_dim.4
  73.3 16.4 %all_to_all.23.sol = f32[16,16,8,128]{3,2,1,0:T(8,128)S(1)} all-to-all(f32[16,16,8,128]{3,2,1,0:T(8,128)S(1)} %broadcast_in_dim.4), channel_id=1, replica_groups=mesh['z'=16,'y'=4,'x'=4,'c'=2] {'y','x'}, dimensions={0} | all-to-all | bytes 2097152 | tf_op jit(solution)/shard_map/all_to_all | solution.py:185
  89.7 6.8 %collective-permute-start.1 = (f32[16,16,8,128]{3,2,1,0:T(8,128)S(1)}, f32[16,16,8,128]{3,2,1,0:T(8,128)S(1)}, u32[]{:S(2)}, u32[]{:S(2)}) collective-permute-start(f32[16,16,8,128]{3,2,1,0:T(8,128)S(1)} %all_to_all.23.sol), channel_id=1, source_target_pairs={{0,1},{1,0},{2,3},{3,2},{4,5},{5,4},{6,7},{7,6},{8,9},{9,8},{10,11... | collective-permute-start | bytes 3145736 | tf_op jit(solution)/shard_map/ppermute | solution.py:186
  96.5 0.0 copy-done
  96.5 0.0 copy-done.1
  96.5 0.0 copy-done.3
  96.5 2.4 %backward_own.1 = (f32[64,256]{1,0:T(8,128)}, f32[512,256]{1,0:T(8,128)}, bf16[24,384,128]{2,1,0:T(8,128)(2,1)S(1)}) custom-call(s32[24]{0:T(128)S(1)} %bitcast.13, f32[512,256]{1,0:T(8,128)S(1)} %bitcast.9, f32[24,128,128]{2,1,0:T(8,128)S(1)} %bitcast.6, f32[16,16,8,128]{3,2,1,0:T(8,128)S(1)} %all_to_all.23.sol), custom_call_target="tpu_custom_call" | custom-call | tf_op jit(solution)/shard_map/backward_own/pallas_call | solution.py:196
  98.9 0.0 collective-permute-done.1.sol
  98.9 2.2 %backward_other.1 = (f32[64,256]{1,0:T(8,128)}, f32[512,256]{1,0:T(8,128)}) custom-call(s32[24]{0:T(128)S(1)} %bitcast.14, f32[512,256]{1,0:T(8,128)S(1)} %bitcast.10, bf16[24,384,128]{2,1,0:T(8,128)(2,1)S(1)} %get-tuple-element.7.weights, f32[16,16,8,128]{3,2,1,0:T(8,128)S(1)} %collective-permute-done.1.sol, ...), custom_call_target="tpu_custom_call", output_to_operand_aliasing={{0}: (4, {}), {1}: (5, {})} | custom-call | tf_op jit(solution)/shard_map/backward_other/pallas_call | solution.py:205
Async XLA Ops:
  3.0 11.2 %collective-permute-start = (f32[16,16,8,128]{3,2,1,0:T(8,128)S(1)}, f32[16,16,8,128]{3,2,1,0:T(8,128)S(1)}, u32[]{:S(2)}, u32[]{:S(2)}) collective-permute-start(f32[16,16,8,128]{3,2,1,0:T(8,128)S(1)} %forward_send.1), channel_id=1, source_target_pairs={{0,1},{1,0},{2,3},{3,2},{4,5},{5,4},{6,7},{7,6},{8,9},{9,8},{10,11... | collective-permute-start | bytes 3145736 | tf_op jit(solution)/shard_map/ppermute | solution.py:171
  14.3 44.3 %copy-start.2 = (f32[1,128,128]{2,1,0:T(8,128)S(1)}, f32[1,128,128]{2,1,0:T(8,128)}, u32[]{:S(2)}) copy-start(f32[1,128,128]{2,1,0:T(8,128)} %pivot.1) | copy-start | bytes 196612
  33.8 62.7 %copy-start = (f32[1,24,128,128]{3,2,1,0:T(8,128)S(1)}, f32[1,24,128,128]{3,2,1,0:T(8,128)}, u32[]{:S(2)}) copy-start(f32[1,24,128,128]{3,2,1,0:T(8,128)} %param.6) | copy-start | bytes 4718596
  33.8 62.7 %copy-start.1 = (f32[1,512,256]{2,1,0:T(8,128)S(1)}, f32[1,512,256]{2,1,0:T(8,128)}, u32[]{:S(2)}) copy-start(f32[1,512,256]{2,1,0:T(8,128)} %param.5) | copy-start | bytes 1572868
  33.8 62.7 %copy-start.3 = (s32[1,24]{1,0:T(1,128)S(1)}, s32[1,24]{1,0:T(1,128)}, u32[]{:S(2)}) copy-start(s32[1,24]{1,0:T(1,128)} %param.7) | copy-start | bytes 292
  89.7 9.2 %collective-permute-start.1 = (f32[16,16,8,128]{3,2,1,0:T(8,128)S(1)}, f32[16,16,8,128]{3,2,1,0:T(8,128)S(1)}, u32[]{:S(2)}, u32[]{:S(2)}) collective-permute-start(f32[16,16,8,128]{3,2,1,0:T(8,128)S(1)} %all_to_all.23.sol), channel_id=1, source_target_pairs={{0,1},{1,0},{2,3},{3,2},{4,5},{5,4},{6,7},{7,6},{8,9},{9,8},{10,11... | collective-permute-start | bytes 3145736 | tf_op jit(solution)/shard_map/ppermute | solution.py:186

commit v4 on v3

--- a/solution.py
+++ b/solution.py
@@ -5,7 +5,7 @@
 from jax import lax
 from jax.experimental import pallas as pl
 from jax.experimental.pallas import tpu as pltpu
-from jax.sharding import Mesh, PartitionSpec as P
+from jax.sharding import PartitionSpec as P
 
 F32 = jnp.float32
 BF16 = jnp.bfloat16
@@ -19,7 +19,14 @@
 
 
 def place():
-    return lax.axis_index("z"), lax.axis_index("y") * lax.axis_size("x") + lax.axis_index("x"), lax.axis_index("c")
+    col = lax.axis_index("col")
+    return lax.axis_index("leaf"), col // 2, col % 2
+
+
+def peer_groups():
+    across = [(i // 4, i % 4) for i in range(16)]
+    stride = [across[3 * i % 16] for i in range(16)]
+    return [[(y * 4 + x) * 2 for y, x in stride], [(x * 4 + y) * 2 + 1 for y, x in stride]]
 
 
 def half_columns(core, size):
@@ -145,8 +152,9 @@
 
 
 def on_device(leaf_solution, coupling, tile_slot, sep_rhs, pivot_inverse):
-    n_z = lax.axis_size("z")
-    n_chip = lax.axis_size("y") * lax.axis_size("x")
+    n_z = lax.axis_size("leaf")
+    n_chip = lax.axis_size("col") // 2
+    groups = peer_groups()
     slots, leaf, tiles, rhs, pivot = tile_slot[0], leaf_solution[0], coupling[0], sep_rhs, in_vmem(pivot_inverse)
     size = tiles.shape[-1]
     leaf_rows, sep_rows = leaf.shape[0], rhs.shape[0]
@@ -167,12 +175,12 @@
             name="forward_send" if swapped else "forward_own",
         )(slots, leaf, tiles, rhs)
 
-    swap = [(0, 1), (1, 0)]
-    arrived = lax.ppermute(forward(True), "c", swap)
+    swap = [(i, i ^ 1) for i in range(2 * n_chip)]
+    arrived = lax.ppermute(forward(True), "col", swap)
     half = forward(False) + arrived
-    shared = lax.all_to_all(half, ("y", "x"), 0, 0, tiled=True)
+    shared = lax.all_to_all(half, "col", 0, 0, axis_index_groups=groups, tiled=True)
     slab = jnp.sum(shared, 0)
-    parts = lax.all_to_all(slab, "z", 0, 0, tiled=True)
+    parts = lax.all_to_all(slab, "leaf", 0, 0, tiled=True)
     copies = pl.pallas_call(
         solve_kernel,
         out_shape=pltpu.VMEM(parts.shape, F32),
@@ -180,10 +188,10 @@
         out_specs=vmem,
         name="solve",
     )(in_vmem(parts), pivot)
-    blocks = lax.all_to_all(copies, "z", 0, 0, tiled=True)
+    blocks = lax.all_to_all(copies, "leaf", 0, 0, tiled=True)
     wide = jnp.broadcast_to(blocks[None], (n_chip,) + blocks.shape)
-    mine = lax.all_to_all(wide, ("y", "x"), 0, 0, tiled=True)
-    other = lax.ppermute(mine, "c", swap)
+    mine = lax.all_to_all(wide, "col", 0, 0, axis_index_groups=groups, tiled=True)
+    other = lax.ppermute(mine, "col", swap)
     scratch = [
         pltpu.VMEM((n_z, size, 3 * size), BF16),
         pltpu.VMEM((col_blocks, size, size), F32),
@@ -216,13 +224,16 @@
 
 
 def solution(mesh):
-    chips = mesh.devices.reshape(mesh.shape["leaf"], 4, mesh.shape["col"] // 8, 2)
-    fine = Mesh(chips, ("z", "y", "x", "c"))
-    col = ("y", "x", "c")
     return jax.shard_map(
         on_device,
-        mesh=fine,
-        in_specs=(P("z", col, None), P("z", col, None, None), P("z", col), P(col, None), P("z", None, None)),
-        out_specs=(P(col, None), P("z", col, None)),
+        mesh=mesh,
+        in_specs=(
+            P("leaf", "col", None),
+            P("leaf", "col", None, None),
+            P("leaf", "col"),
+            P("col", None),
+            P("leaf", None, None),
+        ),
+        out_specs=(P("col", None), P("leaf", "col", None)),
         check_vma=False,
     )

time: 102 us -> 102 us (level)
  blocking collectives: 75 us -> 76.2 us
    all_to_all x4, blocking collectives: 75 us -> 76.2 us  [the longest x1 24.8 us: on_device(): parts = lax.all_to_all(slab, 'leaf', 0, 0, tiled=True)]
where the time goes in v4:
time: 102 us
  blocking collectives  76.2 us (75%)
  starting transfers between devices  14.9 us (15%)
  Pallas kernels  9.51 us (9%)
    all_to_all x1, blocking collectives, on_device(): parts = lax.all_to_all(slab, 'leaf', 0, 0, tiled=True)  24.8 us
    all_to_all x1, blocking collectives, on_device(): lax.all_to_all(half, 'col', 0, 0, axis_index_groups=groups, tiled=True)  19.7 us
    all_to_all x1, blocking collectives, on_device(): lax.all_to_all(wide, 'col', 0, 0, axis_index_groups=groups, tiled=True)  17.3 us
    all_to_all x1, blocking collectives, on_device(): blocks = lax.all_to_all(copies, 'leaf', 0, 0, tiled=True)  14.4 us
    ppermute x1, starting transfers between devices, on_device(): arrived = lax.ppermute(forward(True), 'col', swap)  8.75 us
    ppermute x1, starting transfers between devices, on_device(): other = lax.ppermute(mine, 'col', swap)  6.19 us
    pallas_call x2, Pallas kernels, forward(): pl.pallas_call(partial(forward_kernel, swapped), out_shape=pltpu.VMEM((n_...  4.76 us
    pallas_call x1, Pallas kernels, on_device(): pl.pallas_call(backward_own, out_shape=results + (pltpu.VMEM((tiles.shape...  2.35 us
  transfers between devices with their start and end apart: 2, of which 0 were waited for; matrix products, arithmetic and copies ran while one was open for 0% of the time, Pallas kernels for 5%

profile of v4, /device:TPU:1, one launch (start us, length us, event | category | flops | bytes accessed | tf_op | source)
XLA Modules:
  0.0 101.7 jit_solution(1981158385897125486)
XLA Ops:
  0.6 2.4 %forward_send.1 = f32[16,16,8,128]{3,2,1,0:T(8,128)S(1)} custom-call(s32[24]{0:T(128)} %bitcast.11, f32[512,256]{1,0:T(8,128)} %bitcast.7, f32[24,128,128]{2,1,0:T(8,128)} %bitcast.4, f32[64,256]{1,0:T(8,128)} %rhs_hbm.3), custom_call_target="tpu_custom_call" | custom-call | tf_op jit(solution)/shard_map/forward_send/pallas_call | solution.py:167
  3.0 8.8 %collective-permute-start = (f32[16,16,8,128]{3,2,1,0:T(8,128)S(1)}, f32[16,16,8,128]{3,2,1,0:T(8,128)S(1)}, u32[]{:S(2)}, u32[]{:S(2)}) collective-permute-start(f32[16,16,8,128]{3,2,1,0:T(8,128)S(1)} %forward_send.1), channel_id=1, source_target_pairs={{0,1},{1,0},{2,3},{3,2},{4,5},{5,4},{6,7},{7,6},{8,9},{9,8},{10,11... | collective-permute-start | bytes 3145736 | tf_op jit(solution)/shard_map/ppermute | solution.py:179
  11.8 2.4 %forward_own.1 = f32[16,16,8,128]{3,2,1,0:T(8,128)S(1)} custom-call(s32[24]{0:T(128)} %bitcast.12, f32[512,256]{1,0:T(8,128)} %bitcast.8, f32[24,128,128]{2,1,0:T(8,128)} %bitcast.5, f32[64,256]{1,0:T(8,128)} %rhs_hbm.3), custom_call_target="tpu_custom_call" | custom-call | tf_op jit(solution)/shard_map/forward_own/pallas_call | solution.py:167
  14.2 0.0 collective-permute-done
  14.2 0.1 add.3
  14.3 0.0 copy-start.2
  14.3 19.7 %all_to_all.20 = f32[16,16,8,128]{3,2,1,0:T(8,128)S(1)} all-to-all(f32[16,16,8,128]{3,2,1,0:T(8,128)S(1)} %add.3), channel_id=1, replica_groups={{0,6,12,18,24,30,4,10,16,22,28,2,8,14,20,26},{1,25,19,13,7,31,17,11,5,2..., dimensions={0} | all-to-all | bytes 2097152 | tf_op jit(solution)/shard_map/all_to_all | solution.py:181
  34.1 0.0 copy-start
  34.1 0.0 copy-start.1
  34.1 0.0 copy-start.3
  34.1 0.1 reduce_sum.9
  34.1 24.8 %all_to_all.21.parts = f32[16,8,128]{2,1,0:T(8,128)S(1)} all-to-all(f32[16,8,128]{2,1,0:T(8,128)S(1)} %reduce_sum.9), channel_id=1, replica_groups=mesh['leaf'=16,'col'=32] {'leaf'}, dimensions={0} | all-to-all | bytes 131072 | tf_op jit(solution)/shard_map/all_to_all | solution.py:183
  58.9 0.0 copy-done.2
  58.9 0.2 solve.1
  59.1 14.4 %all_to_all.22 = f32[16,8,128]{2,1,0:T(8,128)S(1)} all-to-all(f32[16,8,128]{2,1,0:T(8,128)S(1)} %solve.1), channel_id=1, replica_groups=mesh['leaf'=16,'col'=32] {'leaf'}, dimensions={0} | all-to-all | bytes 131072 | tf_op jit(solution)/shard_map/all_to_all | solution.py:191
  73.5 0.1 broadcast_in_dim.4
  73.6 17.3 %all_to_all.23.sol = f32[16,16,8,128]{3,2,1,0:T(8,128)S(1)} all-to-all(f32[16,16,8,128]{3,2,1,0:T(8,128)S(1)} %broadcast_in_dim.4), channel_id=1, replica_groups={{0,6,12,18,24,30,4,10,16,22,28,2,8,14,20,26},{1,25,19,13,7,31,17,11,5,2..., dimensions={0} | all-to-all | bytes 2097152 | tf_op jit(solution)/shard_map/all_to_all | solution.py:193
  90.8 6.2 %collective-permute-start.1 = (f32[16,16,8,128]{3,2,1,0:T(8,128)S(1)}, f32[16,16,8,128]{3,2,1,0:T(8,128)S(1)}, u32[]{:S(2)}, u32[]{:S(2)}) collective-permute-start(f32[16,16,8,128]{3,2,1,0:T(8,128)S(1)} %all_to_all.23.sol), channel_id=1, source_target_pairs={{0,1},{1,0},{2,3},{3,2},{4,5},{5,4},{6,7},{7,6},{8,9},{9,8},{10,11... | collective-permute-start | bytes 3145736 | tf_op jit(solution)/shard_map/ppermute | solution.py:194
  97.0 0.0 copy-done
  97.1 0.0 copy-done.1
  97.1 0.0 copy-done.3
  97.1 2.4 %backward_own.1 = (f32[64,256]{1,0:T(8,128)}, f32[512,256]{1,0:T(8,128)}, bf16[24,384,128]{2,1,0:T(8,128)(2,1)S(1)}) custom-call(s32[24]{0:T(128)S(1)} %bitcast.13, f32[512,256]{1,0:T(8,128)S(1)} %bitcast.9, f32[24,128,128]{2,1,0:T(8,128)S(1)} %bitcast.6, f32[16,16,8,128]{3,2,1,0:T(8,128)S(1)} %all_to_all.23.sol), custom_call_target="tpu_custom_call" | custom-call | tf_op jit(solution)/shard_map/backward_own/pallas_call | solution.py:204
  99.4 0.0 collective-permute-done.1.sol
  99.4 2.2 %backward_other.1 = (f32[64,256]{1,0:T(8,128)}, f32[512,256]{1,0:T(8,128)}) custom-call(s32[24]{0:T(128)S(1)} %bitcast.14, f32[512,256]{1,0:T(8,128)S(1)} %bitcast.10, bf16[24,384,128]{2,1,0:T(8,128)(2,1)S(1)} %get-tuple-element.7.weights, f32[16,16,8,128]{3,2,1,0:T(8,128)S(1)} %collective-permute-done.1.sol, ...), custom_call_target="tpu_custom_call", output_to_operand_aliasing={{0}: (4, {}), {1}: (5, {})} | custom-call | tf_op jit(solution)/shard_map/backward_other/pallas_call | solution.py:213
Async XLA Ops:
  3.0 11.2 %collective-permute-start = (f32[16,16,8,128]{3,2,1,0:T(8,128)S(1)}, f32[16,16,8,128]{3,2,1,0:T(8,128)S(1)}, u32[]{:S(2)}, u32[]{:S(2)}) collective-permute-start(f32[16,16,8,128]{3,2,1,0:T(8,128)S(1)} %forward_send.1), channel_id=1, source_target_pairs={{0,1},{1,0},{2,3},{3,2},{4,5},{5,4},{6,7},{7,6},{8,9},{9,8},{10,11... | collective-permute-start | bytes 3145736 | tf_op jit(solution)/shard_map/ppermute | solution.py:179
  14.3 44.6 %copy-start.2 = (f32[1,128,128]{2,1,0:T(8,128)S(1)}, f32[1,128,128]{2,1,0:T(8,128)}, u32[]{:S(2)}) copy-start(f32[1,128,128]{2,1,0:T(8,128)} %pivot.1) | copy-start | bytes 196612
  34.1 63.0 %copy-start = (f32[1,24,128,128]{3,2,1,0:T(8,128)S(1)}, f32[1,24,128,128]{3,2,1,0:T(8,128)}, u32[]{:S(2)}) copy-start(f32[1,24,128,128]{3,2,1,0:T(8,128)} %param.6) | copy-start | bytes 4718596
  34.1 63.0 %copy-start.1 = (f32[1,512,256]{2,1,0:T(8,128)S(1)}, f32[1,512,256]{2,1,0:T(8,128)}, u32[]{:S(2)}) copy-start(f32[1,512,256]{2,1,0:T(8,128)} %param.5) | copy-start | bytes 1572868
  34.1 63.0 %copy-start.3 = (s32[1,24]{1,0:T(1,128)S(1)}, s32[1,24]{1,0:T(1,128)}, u32[]{:S(2)}) copy-start(s32[1,24]{1,0:T(1,128)} %param.7) | copy-start | bytes 292
  90.8 8.6 %collective-permute-start.1 = (f32[16,16,8,128]{3,2,1,0:T(8,128)S(1)}, f32[16,16,8,128]{3,2,1,0:T(8,128)S(1)}, u32[]{:S(2)}, u32[]{:S(2)}) collective-permute-start(f32[16,16,8,128]{3,2,1,0:T(8,128)S(1)} %all_to_all.23.sol), channel_id=1, source_target_pairs={{0,1},{1,0},{2,3},{3,2},{4,5},{5,4},{6,7},{7,6},{8,9},{9,8},{10,11... | collective-permute-start | bytes 3145736 | tf_op jit(solution)/shard_map/ppermute | solution.py:194

commit v5 on v4

--- a/solution.py
+++ b/solution.py
@@ -23,10 +23,10 @@
     return lax.axis_index("leaf"), col // 2, col % 2
 
 
-def peer_groups():
-    across = [(i // 4, i % 4) for i in range(16)]
-    stride = [across[3 * i % 16] for i in range(16)]
-    return [[(y * 4 + x) * 2 for y, x in stride], [(x * 4 + y) * 2 + 1 for y, x in stride]]
+def plane_groups():
+    chips = [((i // 4 + 2) % 4) * 4 + (i + 2) % 4 for i in range(16)]
+    turned = [chip % 4 * 4 + chip // 4 for chip in chips]
+    return [[2 * chip for chip in chips], [2 * chip + 1 for chip in turned]]
 
 
 def half_columns(core, size):
@@ -154,7 +154,7 @@
 def on_device(leaf_solution, coupling, tile_slot, sep_rhs, pivot_inverse):
     n_z = lax.axis_size("leaf")
     n_chip = lax.axis_size("col") // 2
-    groups = peer_groups()
+    groups = plane_groups()
     slots, leaf, tiles, rhs, pivot = tile_slot[0], leaf_solution[0], coupling[0], sep_rhs, in_vmem(pivot_inverse)
     size = tiles.shape[-1]
     leaf_rows, sep_rows = leaf.shape[0], rhs.shape[0]

time: 102 us -> 98 us (0.961)
  blocking collectives: 76.2 us -> 72.6 us
    all_to_all x1, blocking collectives: 24.8 us -> 22.7 us  [on_device(): parts = lax.all_to_all(slab, 'leaf', 0, 0, tiled=True)]
where the time goes in v5:
time: 98 us; the launch traced here: 97.6 us
  blocking collectives  72.6 us (74%)
  starting transfers between devices  14.5 us (15%)
  Pallas kernels  9.52 us (10%)
    all_to_all x1, blocking collectives, on_device(): parts = lax.all_to_all(slab, 'leaf', 0, 0, tiled=True)  22.7 us
    all_to_all x1, blocking collectives, on_device(): lax.all_to_all(half, 'col', 0, 0, axis_index_groups=groups, tiled=True)  19 us
    all_to_all x1, blocking collectives, on_device(): lax.all_to_all(wide, 'col', 0, 0, axis_index_groups=groups, tiled=True)  16.4 us
    all_to_all x1, blocking collectives, on_device(): blocks = lax.all_to_all(copies, 'leaf', 0, 0, tiled=True)  14.5 us
    ppermute x1, starting transfers between devices, on_device(): arrived = lax.ppermute(forward(True), 'col', swap)  8.75 us
    ppermute x1, starting transfers between devices, on_device(): other = lax.ppermute(mine, 'col', swap)  5.76 us
    pallas_call x2, Pallas kernels, forward(): pl.pallas_call(partial(forward_kernel, swapped), out_shape=pltpu.VMEM((n_...  4.78 us
    pallas_call x1, Pallas kernels, on_device(): pl.pallas_call(backward_own, out_shape=results + (pltpu.VMEM((tiles.shape...  2.35 us
  transfers between devices with their start and end apart: 2, of which 0 were waited for; matrix products, arithmetic and copies ran while one was open for 0% of the time, Pallas kernels for 5%

profile of v5, /device:TPU:1, one launch (start us, length us, event | category | flops | bytes accessed | tf_op | source)
XLA Modules:
  0.0 97.6 jit_solution(2207785395663012545)
XLA Ops:
  0.6 2.4 %forward_send.1 = f32[16,16,8,128]{3,2,1,0:T(8,128)S(1)} custom-call(s32[24]{0:T(128)} %bitcast.11, f32[512,256]{1,0:T(8,128)} %bitcast.7, f32[24,128,128]{2,1,0:T(8,128)} %bitcast.4, f32[64,256]{1,0:T(8,128)} %rhs_hbm.3), custom_call_target="tpu_custom_call" | custom-call | tf_op jit(solution)/shard_map/forward_send/pallas_call | solution.py:167
  3.0 8.8 %collective-permute-start = (f32[16,16,8,128]{3,2,1,0:T(8,128)S(1)}, f32[16,16,8,128]{3,2,1,0:T(8,128)S(1)}, u32[]{:S(2)}, u32[]{:S(2)}) collective-permute-start(f32[16,16,8,128]{3,2,1,0:T(8,128)S(1)} %forward_send.1), channel_id=1, source_target_pairs={{0,1},{1,0},{2,3},{3,2},{4,5},{5,4},{6,7},{7,6},{8,9},{9,8},{10,11... | collective-permute-start | bytes 3145736 | tf_op jit(solution)/shard_map/ppermute | solution.py:179
  11.8 2.4 %forward_own.1 = f32[16,16,8,128]{3,2,1,0:T(8,128)S(1)} custom-call(s32[24]{0:T(128)} %bitcast.12, f32[512,256]{1,0:T(8,128)} %bitcast.8, f32[24,128,128]{2,1,0:T(8,128)} %bitcast.5, f32[64,256]{1,0:T(8,128)} %rhs_hbm.3), custom_call_target="tpu_custom_call" | custom-call | tf_op jit(solution)/shard_map/forward_own/pallas_call | solution.py:167
  14.2 0.0 collective-permute-done
  14.2 0.1 add.3
  14.3 0.0 copy-start.2
  14.3 19.0 %all_to_all.20 = f32[16,16,8,128]{3,2,1,0:T(8,128)S(1)} all-to-all(f32[16,16,8,128]{3,2,1,0:T(8,128)S(1)} %add.3), channel_id=1, replica_groups={{20,22,16,18,28,30,24,26,4,6,0,2,12,14,8,10},{21,29,5,13,23,31,7,15,17,..., dimensions={0} | all-to-all | bytes 2097152 | tf_op jit(solution)/shard_map/all_to_all | solution.py:181
  33.3 0.0 copy-start
  33.3 0.0 copy-start.1
  33.3 0.0 copy-start.3
  33.3 0.1 reduce_sum.9
  33.4 22.7 %all_to_all.21.parts = f32[16,8,128]{2,1,0:T(8,128)S(1)} all-to-all(f32[16,8,128]{2,1,0:T(8,128)S(1)} %reduce_sum.9), channel_id=1, replica_groups=mesh['leaf'=16,'col'=32] {'leaf'}, dimensions={0} | all-to-all | bytes 131072 | tf_op jit(solution)/shard_map/all_to_all | solution.py:183
  56.1 0.0 copy-done.2
  56.1 0.2 solve.1
  56.3 14.5 %all_to_all.22 = f32[16,8,128]{2,1,0:T(8,128)S(1)} all-to-all(f32[16,8,128]{2,1,0:T(8,128)S(1)} %solve.1), channel_id=1, replica_groups=mesh['leaf'=16,'col'=32] {'leaf'}, dimensions={0} | all-to-all | bytes 131072 | tf_op jit(solution)/shard_map/all_to_all | solution.py:191
  70.8 0.1 broadcast_in_dim.4
  70.9 16.4 %all_to_all.23.sol = f32[16,16,8,128]{3,2,1,0:T(8,128)S(1)} all-to-all(f32[16,16,8,128]{3,2,1,0:T(8,128)S(1)} %broadcast_in_dim.4), channel_id=1, replica_groups={{20,22,16,18,28,30,24,26,4,6,0,2,12,14,8,10},{21,29,5,13,23,31,7,15,17,..., dimensions={0} | all-to-all | bytes 2097152 | tf_op jit(solution)/shard_map/all_to_all | solution.py:193
  87.2 5.8 %collective-permute-start.1 = (f32[16,16,8,128]{3,2,1,0:T(8,128)S(1)}, f32[16,16,8,128]{3,2,1,0:T(8,128)S(1)}, u32[]{:S(2)}, u32[]{:S(2)}) collective-permute-start(f32[16,16,8,128]{3,2,1,0:T(8,128)S(1)} %all_to_all.23.sol), channel_id=1, source_target_pairs={{0,1},{1,0},{2,3},{3,2},{4,5},{5,4},{6,7},{7,6},{8,9},{9,8},{10,11... | collective-permute-start | bytes 3145736 | tf_op jit(solution)/shard_map/ppermute | solution.py:194
  93.0 0.0 copy-done
  93.0 0.0 copy-done.1
  93.0 0.0 copy-done.3
  93.0 2.3 %backward_own.1 = (f32[64,256]{1,0:T(8,128)}, f32[512,256]{1,0:T(8,128)}, bf16[24,384,128]{2,1,0:T(8,128)(2,1)S(1)}) custom-call(s32[24]{0:T(128)S(1)} %bitcast.13, f32[512,256]{1,0:T(8,128)S(1)} %bitcast.9, f32[24,128,128]{2,1,0:T(8,128)S(1)} %bitcast.6, f32[16,16,8,128]{3,2,1,0:T(8,128)S(1)} %all_to_all.23.sol), custom_call_target="tpu_custom_call" | custom-call | tf_op jit(solution)/shard_map/backward_own/pallas_call | solution.py:204
  95.4 0.0 collective-permute-done.1.sol
  95.4 2.2 %backward_other.1 = (f32[64,256]{1,0:T(8,128)}, f32[512,256]{1,0:T(8,128)}) custom-call(s32[24]{0:T(128)S(1)} %bitcast.14, f32[512,256]{1,0:T(8,128)S(1)} %bitcast.10, bf16[24,384,128]{2,1,0:T(8,128)(2,1)S(1)} %get-tuple-element.7.weights, f32[16,16,8,128]{3,2,1,0:T(8,128)S(1)} %collective-permute-done.1.sol, ...), custom_call_target="tpu_custom_call", output_to_operand_aliasing={{0}: (4, {}), {1}: (5, {})} | custom-call | tf_op jit(solution)/shard_map/backward_other/pallas_call | solution.py:213
Async XLA Ops:
  3.0 11.2 %collective-permute-start = (f32[16,16,8,128]{3,2,1,0:T(8,128)S(1)}, f32[16,16,8,128]{3,2,1,0:T(8,128)S(1)}, u32[]{:S(2)}, u32[]{:S(2)}) collective-permute-start(f32[16,16,8,128]{3,2,1,0:T(8,128)S(1)} %forward_send.1), channel_id=1, source_target_pairs={{0,1},{1,0},{2,3},{3,2},{4,5},{5,4},{6,7},{7,6},{8,9},{9,8},{10,11... | collective-permute-start | bytes 3145736 | tf_op jit(solution)/shard_map/ppermute | solution.py:179
  14.3 41.8 %copy-start.2 = (f32[1,128,128]{2,1,0:T(8,128)S(1)}, f32[1,128,128]{2,1,0:T(8,128)}, u32[]{:S(2)}) copy-start(f32[1,128,128]{2,1,0:T(8,128)} %pivot.1) | copy-start | bytes 196612
  33.3 59.7 %copy-start = (f32[1,24,128,128]{3,2,1,0:T(8,128)S(1)}, f32[1,24,128,128]{3,2,1,0:T(8,128)}, u32[]{:S(2)}) copy-start(f32[1,24,128,128]{3,2,1,0:T(8,128)} %param.6) | copy-start | bytes 4718596
  33.3 59.7 %copy-start.1 = (f32[1,512,256]{2,1,0:T(8,128)S(1)}, f32[1,512,256]{2,1,0:T(8,128)}, u32[]{:S(2)}) copy-start(f32[1,512,256]{2,1,0:T(8,128)} %param.5) | copy-start | bytes 1572868
  33.3 59.7 %copy-start.3 = (s32[1,24]{1,0:T(1,128)S(1)}, s32[1,24]{1,0:T(1,128)}, u32[]{:S(2)}) copy-start(s32[1,24]{1,0:T(1,128)} %param.7) | copy-start | bytes 292
  87.2 8.2 %collective-permute-start.1 = (f32[16,16,8,128]{3,2,1,0:T(8,128)S(1)}, f32[16,16,8,128]{3,2,1,0:T(8,128)S(1)}, u32[]{:S(2)}, u32[]{:S(2)}) collective-permute-start(f32[16,16,8,128]{3,2,1,0:T(8,128)S(1)} %all_to_all.23.sol), channel_id=1, source_target_pairs={{0,1},{1,0},{2,3},{3,2},{4,5},{5,4},{6,7},{7,6},{8,9},{9,8},{10,11... | collective-permute-start | bytes 3145736 | tf_op jit(solution)/shard_map/ppermute | solution.py:194

commit v6 on v5

--- a/solution.py
+++ b/solution.py
@@ -10,6 +10,7 @@
 F32 = jnp.float32
 BF16 = jnp.bfloat16
 CHUNKS = (8, 16)
+FIRST = 10
 
 
 def split(value):
@@ -27,6 +28,10 @@
     chips = [((i // 4 + 2) % 4) * 4 + (i + 2) % 4 for i in range(16)]
     turned = [chip % 4 * 4 + chip // 4 for chip in chips]
     return [[2 * chip for chip in chips], [2 * chip + 1 for chip in turned]]
+
+
+def slot_of(block, count):
+    return (block + count - FIRST) % count
 
 
 def half_columns(core, size):
@@ -59,7 +64,7 @@
     z, chip, core = place()
     count, size = tiles.shape[0], tiles.shape[1]
     col_blocks = leaf.shape[0] // size
-    slabs = out.shape[0]
+    slabs, row_blocks = out.shape[0], out.shape[1]
     cols = half_columns(1 - core if swapped else core, size)
     small, copies = start_copies(
         [(leaf_hbm.at[:, cols], leaf), (slots_hbm, slots), (rhs_hbm.at[:, cols], rhs)], tiles_hbm, tiles, sems
@@ -74,7 +79,7 @@
     lane = lax.broadcasted_iota(jnp.int32, (size, size), 1)
     keep = (lane // (size // 2) == core) & (z == 0)
     placed = jnp.where(keep, jnp.concatenate([rhs[...], rhs[...]], 0).T, 0.0)
-    out[:, chip] = placed.reshape(slabs, 8, size)
+    out[:, slot_of(chip, row_blocks)] = placed.reshape(slabs, 8, size)
 
     def product(t):
         high, low = split(tiles[t])
@@ -82,7 +87,7 @@
         return jnp.dot(lhs[slots[t] % col_blocks], weights, preferred_element_type=F32)
 
     def use(t, value):
-        out[:, slots[t] // col_blocks] -= value.reshape(slabs, 8, size)
+        out[:, slot_of(slots[t] // col_blocks, row_blocks)] -= value.reshape(slabs, 8, size)
 
     pipelined(copies, count, product, use)
 
@@ -107,7 +112,7 @@
     leaf_in.start()
     update[...] = jnp.zeros_like(update)
     rows = sep.shape[0]
-    turned = sol[:, chip].reshape(size, size).T
+    turned = sol[:, slot_of(chip, row_blocks)].reshape(size, size).T
     sep[...] = jnp.where(core == 0, turned[:rows], turned[rows:])
     sep_back.start()
     for k in range(row_blocks):
@@ -116,7 +121,7 @@
     slots_in.wait()
 
     def product(t):
-        return jnp.dot(lhs[slots[t] // col_blocks], weights[t], preferred_element_type=F32)
+        return jnp.dot(lhs[slot_of(slots[t] // col_blocks, row_blocks)], weights[t], preferred_element_type=F32)
 
     ahead = product(0)
     for t in range(count):
@@ -155,6 +160,7 @@
     n_z = lax.axis_size("leaf")
     n_chip = lax.axis_size("col") // 2
     groups = plane_groups()
+    ring = [[(FIRST + i) % n_z for i in range(n_z)]]
     slots, leaf, tiles, rhs, pivot = tile_slot[0], leaf_solution[0], coupling[0], sep_rhs, in_vmem(pivot_inverse)
     size = tiles.shape[-1]
     leaf_rows, sep_rows = leaf.shape[0], rhs.shape[0]
@@ -180,7 +186,7 @@
     half = forward(False) + arrived
     shared = lax.all_to_all(half, "col", 0, 0, axis_index_groups=groups, tiled=True)
     slab = jnp.sum(shared, 0)
-    parts = lax.all_to_all(slab, "leaf", 0, 0, tiled=True)
+    parts = lax.all_to_all(slab, "leaf", 0, 0, axis_index_groups=ring, tiled=True)
     copies = pl.pallas_call(
         solve_kernel,
         out_shape=pltpu.VMEM(parts.shape, F32),
@@ -188,7 +194,7 @@
         out_specs=vmem,
         name="solve",
     )(in_vmem(parts), pivot)
-    blocks = lax.all_to_all(copies, "leaf", 0, 0, tiled=True)
+    blocks = lax.all_to_all(copies, "leaf", 0, 0, axis_index_groups=ring, tiled=True)
     wide = jnp.broadcast_to(blocks[None], (n_chip,) + blocks.shape)
     mine = lax.all_to_all(wide, "col", 0, 0, axis_index_groups=groups, tiled=True)
     other = lax.ppermute(mine, "col", swap)

time: 98 us -> 92.9 us (0.948)
  blocking collectives: 72.6 us -> 67.4 us
    all_to_all x2, blocking collectives: 37.2 us -> 32 us  [the longest x1 17.6 us: on_device(): lax.all_to_all(slab, 'leaf', 0, 0, axis_index_groups=ring, tiled=True)]
where the time goes in v6:
time: 92.9 us; the launch traced here: 92.5 us
  blocking collectives  67.4 us (73%)
  starting transfers between devices  14.5 us (16%)
  Pallas kernels  9.55 us (10%)
    all_to_all x1, blocking collectives, on_device(): lax.all_to_all(half, 'col', 0, 0, axis_index_groups=groups, tiled=True)  19 us
    all_to_all x1, blocking collectives, on_device(): lax.all_to_all(slab, 'leaf', 0, 0, axis_index_groups=ring, tiled=True)  17.6 us
    all_to_all x1, blocking collectives, on_device(): lax.all_to_all(wide, 'col', 0, 0, axis_index_groups=groups, tiled=True)  16.4 us
    all_to_all x1, blocking collectives, on_device(): lax.all_to_all(copies, 'leaf', 0, 0, axis_index_groups=ring, tiled=True)  14.4 us
    ppermute x1, starting transfers between devices, on_device(): arrived = lax.ppermute(forward(True), 'col', swap)  8.75 us
    ppermute x1, starting transfers between devices, on_device(): other = lax.ppermute(mine, 'col', swap)  5.74 us
    pallas_call x2, Pallas kernels, forward(): pl.pallas_call(partial(forward_kernel, swapped), out_shape=pltpu.VMEM((n_...  4.78 us
    pallas_call x1, Pallas kernels, on_device(): pl.pallas_call(backward_own, out_shape=results + (pltpu.VMEM((tiles.shape...  2.36 us
  transfers between devices with their start and end apart: 2, of which 0 were waited for; matrix products, arithmetic and copies ran while one was open for 0% of the time, Pallas kernels for 5%

profile of v6, /device:TPU:1, one launch (start us, length us, event | category | flops | bytes accessed | tf_op | source)
XLA Modules:
  0.0 92.5 jit_solution(7476444974242159663)
XLA Ops:
  0.6 2.4 %forward_send.1 = f32[16,16,8,128]{3,2,1,0:T(8,128)S(1)} custom-call(s32[24]{0:T(128)} %bitcast.11, f32[512,256]{1,0:T(8,128)} %bitcast.7, f32[24,128,128]{2,1,0:T(8,128)} %bitcast.4, f32[64,256]{1,0:T(8,128)} %rhs_hbm.3), custom_call_target="tpu_custom_call" | custom-call | tf_op jit(solution)/shard_map/forward_send/pallas_call | solution.py:173
  3.0 8.8 %collective-permute-start = (f32[16,16,8,128]{3,2,1,0:T(8,128)S(1)}, f32[16,16,8,128]{3,2,1,0:T(8,128)S(1)}, u32[]{:S(2)}, u32[]{:S(2)}) collective-permute-start(f32[16,16,8,128]{3,2,1,0:T(8,128)S(1)} %forward_send.1), channel_id=1, source_target_pairs={{0,1},{1,0},{2,3},{3,2},{4,5},{5,4},{6,7},{7,6},{8,9},{9,8},{10,11... | collective-permute-start | bytes 3145736 | tf_op jit(solution)/shard_map/ppermute | solution.py:185
  11.8 2.4 %forward_own.1 = f32[16,16,8,128]{3,2,1,0:T(8,128)S(1)} custom-call(s32[24]{0:T(128)} %bitcast.12, f32[512,256]{1,0:T(8,128)} %bitcast.8, f32[24,128,128]{2,1,0:T(8,128)} %bitcast.5, f32[64,256]{1,0:T(8,128)} %rhs_hbm.3), custom_call_target="tpu_custom_call" | custom-call | tf_op jit(solution)/shard_map/forward_own/pallas_call | solution.py:173
  14.2 0.0 collective-permute-done
  14.2 0.1 add.3
  14.3 0.0 copy-start.2
  14.3 19.0 %all_to_all.20 = f32[16,16,8,128]{3,2,1,0:T(8,128)S(1)} all-to-all(f32[16,16,8,128]{3,2,1,0:T(8,128)S(1)} %add.3), channel_id=1, replica_groups={{20,22,16,18,28,30,24,26,4,6,0,2,12,14,8,10},{21,29,5,13,23,31,7,15,17,..., dimensions={0} | all-to-all | bytes 2097152 | tf_op jit(solution)/shard_map/all_to_all | solution.py:187
  33.3 0.0 copy-start
  33.4 0.0 copy-start.1
  33.4 0.0 copy-start.3
  33.4 0.1 reduce_sum.9
  33.4 17.6 %all_to_all.21.parts = f32[16,8,128]{2,1,0:T(8,128)S(1)} all-to-all(f32[16,8,128]{2,1,0:T(8,128)S(1)} %reduce_sum.9), channel_id=1, replica_groups={{320,352,384,416,448,480,0,32,64,96,128,160,192,224,256,288},{321,353,3..., dimensions={0} | all-to-all | bytes 131072 | tf_op jit(solution)/shard_map/all_to_all | solution.py:189
  51.0 0.0 copy-done.2
  51.0 0.2 solve.1
  51.2 14.4 %all_to_all.22 = f32[16,8,128]{2,1,0:T(8,128)S(1)} all-to-all(f32[16,8,128]{2,1,0:T(8,128)S(1)} %solve.1), channel_id=1, replica_groups={{320,352,384,416,448,480,0,32,64,96,128,160,192,224,256,288},{321,353,3..., dimensions={0} | all-to-all | bytes 131072 | tf_op jit(solution)/shard_map/all_to_all | solution.py:197
  65.6 0.1 broadcast_in_dim.4
  65.7 16.4 %all_to_all.23.sol = f32[16,16,8,128]{3,2,1,0:T(8,128)S(1)} all-to-all(f32[16,16,8,128]{3,2,1,0:T(8,128)S(1)} %broadcast_in_dim.4), channel_id=1, replica_groups={{20,22,16,18,28,30,24,26,4,6,0,2,12,14,8,10},{21,29,5,13,23,31,7,15,17,..., dimensions={0} | all-to-all | bytes 2097152 | tf_op jit(solution)/shard_map/all_to_all | solution.py:199
  82.1 5.7 %collective-permute-start.1 = (f32[16,16,8,128]{3,2,1,0:T(8,128)S(1)}, f32[16,16,8,128]{3,2,1,0:T(8,128)S(1)}, u32[]{:S(2)}, u32[]{:S(2)}) collective-permute-start(f32[16,16,8,128]{3,2,1,0:T(8,128)S(1)} %all_to_all.23.sol), channel_id=1, source_target_pairs={{0,1},{1,0},{2,3},{3,2},{4,5},{5,4},{6,7},{7,6},{8,9},{9,8},{10,11... | collective-permute-start | bytes 3145736 | tf_op jit(solution)/shard_map/ppermute | solution.py:200
  87.9 0.0 copy-done
  87.9 0.0 copy-done.1
  87.9 0.0 copy-done.3
  87.9 2.4 %backward_own.1 = (f32[64,256]{1,0:T(8,128)}, f32[512,256]{1,0:T(8,128)}, bf16[24,384,128]{2,1,0:T(8,128)(2,1)S(1)}) custom-call(s32[24]{0:T(128)S(1)} %bitcast.13, f32[512,256]{1,0:T(8,128)S(1)} %bitcast.9, f32[24,128,128]{2,1,0:T(8,128)S(1)} %bitcast.6, f32[16,16,8,128]{3,2,1,0:T(8,128)S(1)} %all_to_all.23.sol), custom_call_target="tpu_custom_call" | custom-call | tf_op jit(solution)/shard_map/backward_own/pallas_call | solution.py:210
  90.3 0.0 collective-permute-done.1.sol
  90.3 2.2 %backward_other.1 = (f32[64,256]{1,0:T(8,128)}, f32[512,256]{1,0:T(8,128)}) custom-call(s32[24]{0:T(128)S(1)} %bitcast.14, f32[512,256]{1,0:T(8,128)S(1)} %bitcast.10, bf16[24,384,128]{2,1,0:T(8,128)(2,1)S(1)} %get-tuple-element.7.weights, f32[16,16,8,128]{3,2,1,0:T(8,128)S(1)} %collective-permute-done.1.sol, ...), custom_call_target="tpu_custom_call", output_to_operand_aliasing={{0}: (4, {}), {1}: (5, {})} | custom-call | tf_op jit(solution)/shard_map/backward_other/pallas_call | solution.py:219
Async XLA Ops:
  3.0 11.2 %collective-permute-start = (f32[16,16,8,128]{3,2,1,0:T(8,128)S(1)}, f32[16,16,8,128]{3,2,1,0:T(8,128)S(1)}, u32[]{:S(2)}, u32[]{:S(2)}) collective-permute-start(f32[16,16,8,128]{3,2,1,0:T(8,128)S(1)} %forward_send.1), channel_id=1, source_target_pairs={{0,1},{1,0},{2,3},{3,2},{4,5},{5,4},{6,7},{7,6},{8,9},{9,8},{10,11... | collective-permute-start | bytes 3145736 | tf_op jit(solution)/shard_map/ppermute | solution.py:185
  14.3 36.7 %copy-start.2 = (f32[1,128,128]{2,1,0:T(8,128)S(1)}, f32[1,128,128]{2,1,0:T(8,128)}, u32[]{:S(2)}) copy-start(f32[1,128,128]{2,1,0:T(8,128)} %pivot.1) | copy-start | bytes 196612
  33.3 54.5 %copy-start = (f32[1,24,128,128]{3,2,1,0:T(8,128)S(1)}, f32[1,24,128,128]{3,2,1,0:T(8,128)}, u32[]{:S(2)}) copy-start(f32[1,24,128,128]{3,2,1,0:T(8,128)} %param.6) | copy-start | bytes 4718596
  33.4 54.5 %copy-start.1 = (f32[1,512,256]{2,1,0:T(8,128)S(1)}, f32[1,512,256]{2,1,0:T(8,128)}, u32[]{:S(2)}) copy-start(f32[1,512,256]{2,1,0:T(8,128)} %param.5) | copy-start | bytes 1572868
  33.4 54.5 %copy-start.3 = (s32[1,24]{1,0:T(1,128)S(1)}, s32[1,24]{1,0:T(1,128)}, u32[]{:S(2)}) copy-start(s32[1,24]{1,0:T(1,128)} %param.7) | copy-start | bytes 292
  82.1 8.1 %collective-permute-start.1 = (f32[16,16,8,128]{3,2,1,0:T(8,128)S(1)}, f32[16,16,8,128]{3,2,1,0:T(8,128)S(1)}, u32[]{:S(2)}, u32[]{:S(2)}) collective-permute-start(f32[16,16,8,128]{3,2,1,0:T(8,128)S(1)} %all_to_all.23.sol), channel_id=1, source_target_pairs={{0,1},{1,0},{2,3},{3,2},{4,5},{5,4},{6,7},{7,6},{8,9},{9,8},{10,11... | collective-permute-start | bytes 3145736 | tf_op jit(solution)/shard_map/ppermute | solution.py:200
